TPU v7x, 256 devices: a whole 4x4x8 slice. The times are simulated.
256 devices in a mesh: dp: 8 (over x, core), ctx: 8 (over z), mp: 4 (over y).
Axes of the slice: x: 4, y: 4, z: 8, core: 2. Of those that a mesh axis runs over, the one named last changes fastest.
Arguments:
- inputs: bfloat16 [1, 8192, 2048], P(None, ('dp', 'ctx'), 'mp'), may hold values from -6 to 6
- doc_start: int32 [1, 8192], P(None, ('dp', 'ctx')), may hold values 0 or 1
- gate_weight: bfloat16 [256, 8, 512], P(None, 'mp'), may hold values from -0.375 to 0.375
- gate_bias: float32 [8, 512], P('mp'), may hold values from -4 to 4
- decay_rate: float32 [2048], P('mp'), may hold values from 2.4414063e-06 to 0.08, as said below
- cotangent: bfloat16 [1, 8192, 2048], P(None, ('dp', 'ctx'), 'mp'), may hold values from -0.59765625 to 0.59765625
Outputs:
- outputs: bfloat16 [1, 8192, 2048], P(None, ('dp', 'ctx'), 'mp')
- grad_inputs: bfloat16 [1, 8192, 2048], P(None, ('dp', 'ctx'), 'mp')
- grad_gate_weight: float32 [256, 8, 512], P(('dp', 'ctx'), 'mp')
Inputs may be any that keep to these rules, and one draw needn't show every extreme that they name: `decay_rate`: each channel's rate is either slow, between 0.02 / 8192 and 0.2 / 8192, or fast, between 0.02 and 0.08, in any mix.
All inputs are finite; a program needn't handle non-finite values. No bound on the sum of `doc_start` on one device may be relied on, other than what follows from the above.
Results may differ from a plain program's by a relative error of at most 0.0028.
Values sent between devices are 32-bit elements; how exact they have to be, the bound alone decides.
No kernel may reach another device: no remote copies, remote signals or barrier semaphores. Data moves between devices by JAX's collectives and lax.ppermute only.
A program may use at most 64 MiB of HBM per device.

v0:
```python
import jax
import jax.numpy as jnp
from jax import lax
from jax.experimental import pallas as pl
from jax.experimental.pallas import tpu as pltpu
from jax.sharding import Mesh, PartitionSpec as P

LANES = 128
SUB = 8


def column_scan(decays, drives, backward):
    rows = decays.shape[0]
    groups = rows // SUB
    a = decays.reshape(groups, SUB, LANES)
    b = drives.reshape(groups, SUB, LANES)
    place = lax.broadcasted_iota(jnp.int32, (groups, SUB, LANES), 1)
    step = 1
    while step < SUB:
        if backward:
            shift, ok = SUB - step, place < SUB - step
        else:
            shift, ok = step, place >= step
        a_far = jnp.where(ok, pltpu.roll(a, shift, 1), 1.0)
        b_far = jnp.where(ok, pltpu.roll(b, shift, 1), 0.0)
        b = a * b_far + b
        a = a * a_far
        step *= 2
    order = range(groups - 1, -1, -1) if backward else range(groups)
    edge = 0 if backward else SUB - 1
    a_in = jnp.ones((1, LANES), jnp.float32)
    b_in = jnp.zeros((1, LANES), jnp.float32)
    a_out, b_out = [None] * groups, [None] * groups
    for g in order:
        a_out[g] = a[g] * a_in
        b_out[g] = a[g] * b_in + b[g]
        a_in = a_out[g][edge : edge + 1]
        b_in = b_out[g][edge : edge + 1]
    return jnp.concatenate(a_out, 0), jnp.concatenate(b_out, 0), a_in, b_in


def local_kernel(
    x_ref, doc_ref, w_ref, bias_ref, rate_ref, cot_ref,
    summary_ref, k1_ref, k2_ref, k3_ref, k4_ref, cum_ref, ls_ref, pc_ref, la_ref,
):
    rows, width = x_ref.shape
    heads, head_dim, _ = w_ref.shape
    doc = jnp.broadcast_to(doc_ref[...].astype(jnp.float32), (LANES, rows))
    keep = 1.0 - jnp.transpose(doc)
    row = lax.broadcasted_iota(jnp.int32, (rows, LANES), 0)
    for h in range(heads):
        pre = jnp.dot(
            x_ref[:, h * head_dim : (h + 1) * head_dim], w_ref[h], preferred_element_type=jnp.float32
        ) + bias_ref[h : h + 1, :]
        for part in range(head_dim // LANES):
            q = h * (head_dim // LANES) + part
            lanes = slice(q * LANES, (q + 1) * LANES)
            rgate = jax.nn.sigmoid(pre[:, part * LANES : (part + 1) * LANES])
            igate = jax.nn.sigmoid(pre[:, head_dim + part * LANES : head_dim + (part + 1) * LANES])
            x = x_ref[:, lanes].astype(jnp.float32)
            rate8 = -8.0 * rate_ref[:, lanes]
            decay = jnp.exp(rate8 * rgate)
            carry = decay * keep
            square = decay * decay
            root = jnp.sqrt(1.0 - square + 0.01)
            kept = keep > 0.5
            scale = jnp.where(kept, root, 1.0)
            dscale = jnp.where(kept, -square / root, 0.0)
            slope = rate8 * (rgate * (1.0 - rgate))
            k4 = scale * igate
            drive = k4 * x
            k1_ref[:, lanes] = carry * slope
            k2_ref[:, lanes] = igate * x * dscale * slope
            k3_ref[:, lanes] = drive * (1.0 - igate)
            k4_ref[:, lanes] = k4
            cum, state, product, last = column_scan(carry, drive, False)
            cum_ref[:, lanes] = cum
            ls_ref[:, lanes] = state
            cot = cot_ref[:, lanes].astype(jnp.float32)
            ahead = jnp.where(row == rows - 1, 1.0, pltpu.roll(carry, rows - 1, 0))
            pc, adjoint, _, first = column_scan(ahead, cot, True)
            pc_ref[:, lanes] = pc
            la_ref[:, lanes] = adjoint
            summary_ref[0, q : q + 1, :] = product
            summary_ref[1, q : q + 1, :] = last
            summary_ref[2, q : q + 1, :] = carry[0:1] * first


def finish_kernel(
    place_ref, all_ref, x_ref, w_ref, k1_ref, k2_ref, k3_ref, k4_ref, cum_ref, ls_ref, pc_ref, la_ref,
    out_ref, gx_ref, mine_ref, other_ref, gw_ref,
):
    rows, width = x_ref.shape
    heads, head_dim, _ = w_ref.shape
    mine, core = place_ref[0], place_ref[1]
    count = all_ref.shape[0]
    entering = jnp.zeros(all_ref.shape[2:], jnp.float32)
    arriving = entering
    for j in range(count - 1):
        entering = jnp.where(j < mine, all_ref[j, 0] * entering + all_ref[j, 1], entering)
        i = count - 1 - j
        arriving = jnp.where(i > mine, all_ref[i, 0] * arriving + all_ref[i, 2], arriving)
    row = lax.broadcasted_iota(jnp.int32, (rows, LANES), 0)
    parts = head_dim // LANES
    for h in range(heads):
        gate, drive, direct = [], [], []
        for part in range(parts):
            q = h * parts + part
            lanes = slice(q * LANES, (q + 1) * LANES)
            before = entering[q : q + 1]
            state = ls_ref[:, lanes] + cum_ref[:, lanes] * before
            out_ref[:, lanes] = state.astype(jnp.bfloat16)
            previous = jnp.where(row == 0, before, pltpu.roll(state, 1, 0))
            adjoint = la_ref[:, lanes] + pc_ref[:, lanes] * arriving[q : q + 1]
            gate.append((adjoint * (k1_ref[:, lanes] * previous + k2_ref[:, lanes])).astype(jnp.bfloat16))
            drive.append((adjoint * k3_ref[:, lanes]).astype(jnp.bfloat16))
            direct.append(adjoint * k4_ref[:, lanes])
        dpre = jnp.concatenate(gate + drive, axis=1)
        back = lax.dot_general(dpre, w_ref[h], (((1,), (1,)), ((), ())), preferred_element_type=jnp.float32)
        columns = slice(h * head_dim, (h + 1) * head_dim)
        gx_ref[:, columns] = (jnp.concatenate(direct, axis=1) + back).astype(jnp.bfloat16)
        gw_ref[:, h * 2 * head_dim : (h + 1) * 2 * head_dim] = lax.dot_general(
            x_ref[:, columns], dpre, (((0,), (0,)), ((), ())), preferred_element_type=jnp.float32
        )
    chunks, depth = mine_ref.shape[0], mine_ref.shape[1]
    for c in range(chunks):
        start = pl.multiple_of(c * 2 * depth + core * depth, depth)
        mine_ref[c] = gw_ref[pl.ds(start, depth), :]
        start = pl.multiple_of(c * 2 * depth + (1 - core) * depth, depth)
        other_ref[c] = gw_ref[pl.ds(start, depth), :]


def per_device(inputs, doc_start, gate_weight, gate_bias, decay_rate, cotangent):
    _, rows, width = inputs.shape
    head_dim, heads, wide = gate_weight.shape
    n_x, n_core, n_z = lax.axis_size("x"), lax.axis_size("core"), lax.axis_size("z")
    blocks = n_x * n_core * n_z
    x = inputs.reshape(rows, width)
    weight = jnp.moveaxis(gate_weight, 1, 0)
    f32 = jnp.float32
    field = jax.ShapeDtypeStruct((rows, width), f32)
    params = pltpu.CompilerParams(vmem_limit_bytes=24 << 20)
    tiles = width // LANES
    summary, *saved = pl.pallas_call(
        local_kernel,
        out_shape=[jax.ShapeDtypeStruct((3, tiles, LANES), f32)] + [field] * 8,
        compiler_params=params,
        name="local_scans",
    )(x, doc_start, weight, gate_bias, decay_rate.reshape(1, width), cotangent.reshape(rows, width))
    spread = jnp.broadcast_to(summary, (blocks,) + summary.shape)
    everyone = lax.all_to_all(spread, ("x", "core", "z"), 0, 0)
    core = lax.axis_index("core")
    place = jnp.stack([(lax.axis_index("x") * n_core + core) * n_z + lax.axis_index("z"), core])
    vmem = pl.BlockSpec(memory_space=pltpu.VMEM)
    depth = head_dim // (n_x * n_core)
    half = jax.ShapeDtypeStruct((n_x, depth, heads * wide), f32)
    outputs, grad_inputs, mine, other = pl.pallas_call(
        finish_kernel,
        out_shape=[
            jax.ShapeDtypeStruct((rows, width), jnp.bfloat16),
            jax.ShapeDtypeStruct((rows, width), jnp.bfloat16),
            half,
            half,
        ],
        in_specs=[pl.BlockSpec(memory_space=pltpu.SMEM)] + [vmem] * 11,
        scratch_shapes=[pltpu.VMEM((head_dim, heads * wide), f32)],
        compiler_params=params,
        name="finish",
    )(place, everyone, x, weight, *saved)
    swapped = lax.ppermute(other, "core", [(0, 1), (1, 0)])
    pair = (mine + swapped).reshape(n_x * n_z, depth // n_z, heads * wide)
    pieces = lax.all_to_all(pair, ("x", "z"), 0, 0)
    grad_gate_weight = pieces.sum(0).reshape(depth // n_z, heads, wide)
    return (outputs[None], grad_inputs[None], grad_gate_weight)


def solution(mesh):
    n_dp, n_ctx, n_mp = mesh.devices.shape
    fine = Mesh(mesh.devices.reshape(n_dp // 2, 2, n_ctx, n_mp), ("x", "core", "z", "mp"))
    place = ("x", "core", "z")
    return jax.shard_map(
        per_device,
        mesh=fine,
        in_specs=(P(None, place, "mp"), P(None, place), P(None, "mp", None), P("mp", None), P("mp"), P(None, place, "mp")),
        out_specs=(P(None, place, "mp"), P(None, place, "mp"), P(place, "mp", None)),
        check_vma=False,
    )
```

profile of v0, /device:TPU:56, one launch (start us, length us, event | category | flops | bytes accessed | tf_op | source)
XLA Modules:
  0.0 58.8 jit_solution(705036425093072746)
XLA Ops:
  0.6 0.0 copy-start.1
  0.6 0.0 copy-start
  0.7 1.1 %copy.11 = bf16[256,2,512]{2,0,1:T(8,128)(2,1)S(1)} copy(bf16[256,2,512]{2,1,0:T(2,128)(2,1)} %param.8) | data formatting | bytes 1048576 | tf_op args[2]
  1.8 0.0 copy-start.2
  1.8 0.0 copy-start.3
  1.8 0.0 copy-start.4
  1.8 0.0 copy-done.1
  1.8 0.0 copy-done
  1.8 0.6 %copy-done.2 = f32[2,512]{1,0:T(2,128)S(1)} copy-done((f32[2,512]{1,0:T(2,128)S(1)}, f32[2,512]{1,0:T(2,128)}, u32[]{:S(2)}) %copy-start.2) | copy-done | bytes 4120
  2.5 0.0 copy-done.3
  2.5 0.0 copy-done.4
  2.5 1.0 %local_scans.1 = (f32[3,4,128]{2,1,0:T(4,128)S(1)}, f32[128,512]{1,0:T(8,128)S(1)}, f32[128,512]{1,0:T(8,128)S(1)}, f32[128,512]{1,0:T(8,128)S(1)}, f32[128,512]...) custom-call(bf16[128,512]{1,0:T(8,128)(2,1)S(1)} %bitcast.12, ...), custom_call_target="tpu_custom_call" | custom-call | tf_op jit(solution)/shard_map/local_scans/pallas_call | solution.py:144
  3.5 0.8 %broadcast_in_dim.9 = f32[64,3,4,128]{3,2,1,0:T(4,128)} broadcast(f32[3,4,128]{2,1,0:T(4,128)S(1)} %get-tuple-element.16), dimensions={1,2,3} | broadcast | bytes 399360 | tf_op jit(solution)/shard_map/broadcast_in_dim | solution.py:150
  4.3 11.6 %all-to-all-start = ((f32[64,3,4,128]{3,2,1,0:T(4,128)}), f32[64,3,4,128]{3,2,1,0:T(4,128)S(1)}, u32[]{:S(2)}, u32[]{:S(2)}) async-start(f32[64,3,4,128]{3,2,1,0:T(4,128)} %broadcast_in_dim.9), calls=%async_computation | async-start | bytes 786432 | tf_op jit(solution)/shard_map/all_to_all | solution.py:151
  15.9 0.1 pad_add_fusion.place_ref
  16.0 15.1 %all-to-all-done.all_ref = f32[64,3,4,128]{3,2,1,0:T(4,128)S(1)} async-done(((f32[64,3,4,128]{3,2,1,0:T(4,128)}), f32[64,3,4,128]{3,2,1,0:T(4,128)S(1)}, u32[]{:S(2)}, u32[]{:S(2)}) %all-to-all-start) | async-done | bytes 393248 | tf_op jit(solution)/shard_map/all_to_all | solution.py:151
  31.0 1.8 %finish.1 = (bf16[128,512]{1,0:T(8,128)(2,1)}, bf16[128,512]{1,0:T(8,128)(2,1)}, f32[4,32,1024]{2,1,0:T(8,128)S(1)}, f32[4,32,1024]{2,1,0:T(8,128)S(1)}) custom-call(s32[2]{0:T(128)S(1)} %pad_add_fusion.place_ref, f32[64,3,4,128]{3,2,1,0:T(4,128)S(1)} %all-to-all-done.all_ref, bf16[128,512]{1,0:T(8,128)(2,1)S(1)} %bitcast.13, ...), custom_call_target="tpu_custom_call" | custom-call | tf_op jit(solution)/shard_map/finish/pallas_call | solution.py:157
  32.9 0.0 collective-permute-start
  32.9 1.9 %collective-permute-done = f32[4,32,1024]{2,1,0:T(8,128)S(1)} collective-permute-done((f32[4,32,1024]{2,1,0:T(8,128)S(1)}, f32[4,32,1024]{2,1,0:T(8,128)S(1)}, u32[]{:S(2)}, u32[]{:S(2)}) %collective-permute-start) | collective-permute-done | bytes 524320 | tf_op jit(solution)/shard_map/ppermute | solution.py:170
  34.8 0.1 add.11
  34.8 0.1 reshape.24
  35.0 23.0 %all_to_all.10 = f32[32,4,1024]{2,1,0:T(4,128)S(1)} all-to-all(f32[32,4,1024]{2,1,0:T(4,128)S(1)} %reshape.24), channel_id=1, replica_groups=mesh['x'=4,'core'=2,'z'=8,'mp'=4] {'x','z'}, dimensions={0} | all-to-all | bytes 1048576 | tf_op jit(solution)/shard_map/all_to_all | solution.py:172
  58.0 0.1 reduce_sum.9
  58.1 0.6 %reshape.25 = f32[4,2,512]{2,1,0:T(2,128)} reshape(f32[4,1024]{1,0:T(4,128)S(1)} %reduce_sum.9) | data formatting | bytes 32768 | tf_op jit(solution)/shard_map/reshape | solution.py:173
Async XLA Ops:
  0.6 1.2 %copy-start.1 = (bf16[1,128,512]{2,1,0:T(8,128)(2,1)S(1)}, bf16[1,128,512]{2,1,0:T(8,128)(2,1)}, u32[]{:S(2)}) copy-start(bf16[1,128,512]{2,1,0:T(8,128)(2,1)} %param.11) | copy-start | bytes 393220
  0.6 1.2 %copy-start = (bf16[1,128,512]{2,1,0:T(8,128)(2,1)S(1)}, bf16[1,128,512]{2,1,0:T(8,128)(2,1)}, u32[]{:S(2)}) copy-start(bf16[1,128,512]{2,1,0:T(8,128)(2,1)} %param.6) | copy-start | bytes 393220
  1.8 0.7 %copy-start.2 = (f32[2,512]{1,0:T(2,128)S(1)}, f32[2,512]{1,0:T(2,128)}, u32[]{:S(2)}) copy-start(f32[2,512]{1,0:T(2,128)} %bias_ref.1) | copy-start | bytes 12292
  1.8 0.7 %copy-start.3 = (f32[512]{0:T(512)S(1)}, f32[512]{0:T(512)}, u32[]{:S(2)}) copy-start(f32[512]{0:T(512)} %param.10) | copy-start | bytes 6148
  1.8 0.7 %copy-start.4 = (s32[1,128]{1,0:T(1,128)S(1)}, s32[1,128]{1,0:T(1,128)}, u32[]{:S(2)}) copy-start(s32[1,128]{1,0:T(1,128)} %doc_ref.1) | copy-start | bytes 1540
  4.3 26.8 %all-to-all-start = ((f32[64,3,4,128]{3,2,1,0:T(4,128)}), f32[64,3,4,128]{3,2,1,0:T(4,128)S(1)}, u32[]{:S(2)}, u32[]{:S(2)}) async-start(f32[64,3,4,128]{3,2,1,0:T(4,128)} %broadcast_in_dim.9), calls=%async_computation | async-start | bytes 786432 | tf_op jit(solution)/shard_map/all_to_all | solution.py:151
  32.9 1.9 %collective-permute-start = (f32[4,32,1024]{2,1,0:T(8,128)S(1)}, f32[4,32,1024]{2,1,0:T(8,128)S(1)}, u32[]{:S(2)}, u32[]{:S(2)}) collective-permute-start(f32[4,32,1024]{2,1,0:T(8,128)S(1)} %get-tuple-element.28), channel_id=1, source_target_pairs={{0,32},{32,0},{1,33},{33,1},{2,34},{34,2},{3,35},{35,3},{4,36},{36... | collective-permute-start | bytes 1572872 | tf_op jit(solution)/shard_map/ppermute | solution.py:170
where the time goes:
time: 59 us; the launch traced here: 58.8 us
  blocking collectives  23 us (39%)
  waiting for transfers between devices  17 us (29%)
  starting transfers between devices  11.6 us (20%)
  local copies, waits for them, and re-layouts  3.38 us (6%)
  Pallas kernels  2.79 us (5%)
  between operations  0.72 us (1%)
    all_to_all x1, blocking collectives, per_device(): pieces = lax.all_to_all(pair, ('x', 'z'), 0, 0)  23 us
    all_to_all x1, waiting for transfers between devices, per_device(): everyone = lax.all_to_all(spread, ('x', 'core', 'z'), 0, 0)  15.1 us
    all_to_all x1, starting transfers between devices, per_device(): everyone = lax.all_to_all(spread, ('x', 'core', 'z'), 0, 0)  11.6 us
    ppermute x1, waiting for transfers between devices, per_device(): swapped = lax.ppermute(other, 'core', [(0, 1), (1, 0)])  1.91 us
    pallas_call x1, Pallas kernels, per_device(): pl.pallas_call(finish_kernel, out_shape=[jax.ShapeDtypeStruct((rows, widt...  1.81 us
    unnamed x11, local copies, waits for them, and re-layouts  1.8 us
  transfers between devices with their start and end apart: 2, of which 2 were waited for; matrix products, arithmetic and copies ran while one was open for 0% of the time, Pallas kernels for 0%

commit v1 on v0

v1 whole, which is shorter than its diff:
```python
import jax
import jax.numpy as jnp
from jax import lax
from jax.experimental import pallas as pl
from jax.experimental.pallas import tpu as pltpu
from jax.sharding import Mesh, PartitionSpec as P

LANES = 128
SUB = 8
F32 = jnp.float32
BF16 = jnp.bfloat16


def column_scan(decays, drives, backward):
    rows = decays.shape[0]
    groups = rows // SUB
    a = decays.reshape(groups, SUB, LANES)
    b = drives.reshape(groups, SUB, LANES)
    place = lax.broadcasted_iota(jnp.int32, (groups, SUB, LANES), 1)
    step = 1
    while step < SUB:
        if backward:
            shift, ok = SUB - step, place < SUB - step
        else:
            shift, ok = step, place >= step
        a_far = jnp.where(ok, pltpu.roll(a, shift, 1), 1.0)
        b_far = jnp.where(ok, pltpu.roll(b, shift, 1), 0.0)
        b = a * b_far + b
        a = a * a_far
        step *= 2
    order = range(groups - 1, -1, -1) if backward else range(groups)
    edge = 0 if backward else SUB - 1
    a_in = jnp.ones((1, LANES), F32)
    b_in = jnp.zeros((1, LANES), F32)
    a_out, b_out = [None] * groups, [None] * groups
    for g in order:
        a_out[g] = a[g] * a_in
        b_out[g] = a[g] * b_in + b[g]
        a_in = a_out[g][edge : edge + 1]
        b_in = b_out[g][edge : edge + 1]
    return jnp.concatenate(a_out, 0), jnp.concatenate(b_out, 0), a_in, b_in


def pack_kernel(x_ref, cot_ref, doc_ref, _, send_ref, own_ref):
    rows, width = x_ref.shape
    half = width // 2
    first = lax.axis_index("core") == 0
    for r, ref in enumerate((x_ref, cot_ref)):
        both = ref[...].astype(F32)
        send_ref[r * rows : (r + 1) * rows, :] = jnp.where(first, both[:, half:], both[:, :half])
        own_ref[r * rows : (r + 1) * rows, :] = jnp.where(first, both[:, :half], both[:, half:])
    doc = jnp.broadcast_to(doc_ref[...].astype(F32), (SUB, rows))
    doc = jnp.concatenate([doc] * (half // rows), axis=1)
    send_ref[2 * rows : 2 * rows + SUB, :] = doc
    own_ref[2 * rows : 2 * rows + SUB, :] = doc


def local_scans(pack_ref, w_ref, bias_ref, rate_ref, x_ref, k1_ref, k2_ref, k3_ref, k4_ref, cum_ref, ls_ref, pc_ref, la_ref):
    rows, half = x_ref.shape
    core = lax.axis_index("core")
    row = lax.broadcasted_iota(jnp.int32, (rows, LANES), 0)
    x_ref[...] = pack_ref[:rows].astype(BF16)
    rate8 = -8.0 * jnp.where(core == 0, rate_ref[:, :half], rate_ref[:, half:])
    pre = jnp.dot(x_ref[...], w_ref[core], preferred_element_type=F32) + bias_ref[pl.ds(core, 1), :]
    keep = 1.0 - jnp.transpose(jnp.broadcast_to(pack_ref[2 * rows : 2 * rows + 1, :rows], (LANES, rows)))
    kept = keep > 0.5
    ends = []
    for part in range(half // LANES):
        lanes = slice(part * LANES, (part + 1) * LANES)
        rgate = jax.nn.sigmoid(pre[:, lanes])
        igate = jax.nn.sigmoid(pre[:, half + part * LANES : half + (part + 1) * LANES])
        x = pack_ref[:rows, lanes]
        rate = rate8[:, lanes]
        decay = jnp.exp(rate * rgate)
        carry = decay * keep
        square = decay * decay
        root = jnp.sqrt(1.0 - square + 0.01)
        scale = jnp.where(kept, root, 1.0)
        dscale = jnp.where(kept, -square / root, 0.0)
        slope = rate * (rgate * (1.0 - rgate))
        k4 = scale * igate
        drive = k4 * x
        k1_ref[:, lanes] = carry * slope
        k2_ref[:, lanes] = igate * x * dscale * slope
        k3_ref[:, lanes] = drive * (1.0 - igate)
        k4_ref[:, lanes] = k4
        cum, state, product, last = column_scan(carry, drive, False)
        cum_ref[:, lanes] = cum
        ls_ref[:, lanes] = state
        ahead = jnp.where(row == rows - 1, 1.0, pltpu.roll(carry, rows - 1, 0))
        pc, adjoint, _, top = column_scan(ahead, pack_ref[rows : 2 * rows, lanes], True)
        pc_ref[:, lanes] = pc
        la_ref[:, lanes] = adjoint
        ends.append((product, last, carry[0:1] * top))
    return ends


def own_kernel(pack_ref, w_ref, bias_ref, rate_ref, summary_ref, *refs):
    for part, values in enumerate(local_scans(pack_ref, w_ref, bias_ref, rate_ref, *refs)):
        for i, value in enumerate(values):
            summary_ref[i, part : part + 1, :] = value


def got_kernel(pack_ref, w_ref, bias_ref, rate_ref, own_ref, spread_ref, *refs):
    *refs, summary_ref = refs
    core = lax.axis_index("core")
    ends = local_scans(pack_ref, w_ref, bias_ref, rate_ref, *refs)
    for part, values in enumerate(ends):
        for i, value in enumerate(values):
            summary_ref[i, pl.ds(core * len(ends) + part, 1), :] = own_ref[i, part : part + 1, :]
            summary_ref[i, pl.ds((1 - core) * len(ends) + part, 1), :] = value
    summary = summary_ref[...]
    for j in range(spread_ref.shape[0]):
        spread_ref[j] = summary


def fold(all_ref, order, kind, base, wanted=None):
    product = jnp.ones(all_ref.shape[2:], F32)
    value = jnp.zeros(all_ref.shape[2:], F32)
    for z in order:
        a, b = all_ref[base + z, 0], all_ref[base + z, kind]
        if wanted is not None:
            a, b = jnp.where(wanted(z), a, 1.0), jnp.where(wanted(z), b, 0.0)
        value = a * value + b
        product = product * a
    return product, value


def edges(all_ref, kind, x, z, n_x, n_z, backward):
    half = all_ref.shape[2] // 2
    cores = (slice(0, half), slice(half, 2 * half))
    near, far = (cores[1], cores[0]) if backward else cores
    order = range(n_z - 1, -1, -1) if backward else range(n_z)
    apply = lambda link, at, value: link[0][at] * value + link[1][at]
    carried = jnp.zeros((half, LANES), F32)
    for i in range(n_x - 1, 0, -1) if backward else range(n_x - 1):
        link = fold(all_ref, order, kind, i * n_z)
        carried = jnp.where(i > x if backward else i < x, apply(link, far, apply(link, near, carried)), carried)
    base = x * n_z
    whole = fold(all_ref, order, kind, base)
    partial = fold(all_ref, order, kind, base, (lambda i: i > z) if backward else (lambda i: i < z))
    ahead = apply(partial, near, carried)
    behind = apply(partial, far, apply(whole, near, carried))
    return (behind, ahead) if backward else (ahead, behind)


def finish_kernel(n_x, n_z, all_ref, *refs):
    own, got, (out_ref, send_ref, dpre_ref, direct_ref, gw_ref) = refs[:9], refs[9:18], refs[18:]
    rows, half = out_ref.shape
    first = lax.axis_index("core") == 0
    at_x, at_z = lax.axis_index("x"), lax.axis_index("z")
    entering = edges(all_ref, 1, at_x, at_z, n_x, n_z, False)
    arriving = edges(all_ref, 2, at_x, at_z, n_x, n_z, True)
    row = lax.broadcasted_iota(jnp.int32, (rows, LANES), 0)
    weight_grad = 0.0
    for block, (x_ref, k1_ref, k2_ref, k3_ref, k4_ref, cum_ref, ls_ref, pc_ref, la_ref) in enumerate((own, got)):
        there = slice(block * rows, (block + 1) * rows)
        before = jnp.where(first, entering[block], entering[1 - block])
        after = jnp.where(first, arriving[block], arriving[1 - block])
        for part in range(half // LANES):
            lanes = slice(part * LANES, (part + 1) * LANES)
            start = before[part : part + 1]
            state = ls_ref[:, lanes] + cum_ref[:, lanes] * start
            if block == 0:
                out_ref[:, lanes] = state.astype(BF16)
            else:
                send_ref[:, lanes] = state
            previous = jnp.where(row == 0, start, pltpu.roll(state, 1, 0))
            adjoint = la_ref[:, lanes] + pc_ref[:, lanes] * after[part : part + 1]
            dpre_ref[there, lanes] = (adjoint * (k1_ref[:, lanes] * previous + k2_ref[:, lanes])).astype(BF16)
            far = slice(half + part * LANES, half + (part + 1) * LANES)
            dpre_ref[there, far] = (adjoint * k3_ref[:, lanes]).astype(BF16)
            direct_ref[there, lanes] = adjoint * k4_ref[:, lanes]
        weight_grad = weight_grad + lax.dot_general(
            x_ref[...], dpre_ref[there, :], (((0,), (0,)), ((), ())), preferred_element_type=F32
        )
    depth = SUB // 2
    low = lax.broadcasted_iota(jnp.int32, (SUB, 2 * half), 0) < depth
    for i in range(n_x):
        for pair in range(n_z // 2):
            u = weight_grad[i * 2 * n_z * depth + pair * SUB :][:SUB]
            v = weight_grad[(i * 2 + 1) * n_z * depth + pair * SUB :][:SUB]
            gw_ref[i * n_z + 2 * pair] = jnp.where(low, u, pltpu.roll(v, depth, 0))
            gw_ref[i * n_z + 2 * pair + 1] = jnp.where(low, pltpu.roll(u, depth, 0), v)


def inputs_kernel(dpre_ref, direct_ref, w_ref, states_ref, gx_ref, send_ref):
    rows = gx_ref.shape[0]
    core = lax.axis_index("core")
    back = lax.dot_general(dpre_ref[...], w_ref[core], (((1,), (1,)), ((), ())), preferred_element_type=F32)
    total = direct_ref[...] + back
    gx_ref[...] = total[:rows].astype(BF16)
    send_ref[:rows] = states_ref[...]
    send_ref[rows:] = total[rows:]


def unswap_kernel(out_ref, gx_ref, got_ref, outputs_ref, grad_ref, order_ref):
    rows, half = out_ref.shape
    first = lax.axis_index("core") == 0
    for r, (own, whole) in enumerate(((out_ref, outputs_ref), (gx_ref, grad_ref))):
        mine = own[...].astype(F32)
        got = got_ref[r * rows : (r + 1) * rows]
        whole[:, :half] = jnp.where(first, mine, got).astype(BF16)
        whole[:, half:] = jnp.where(first, got, mine).astype(BF16)
    order_ref[...] = jnp.zeros_like(order_ref)


def sum_kernel(pieces_ref, _, keep_ref, send_ref):
    total = pieces_ref[0]
    for j in range(1, pieces_ref.shape[0]):
        total = total + pieces_ref[j]
    first = lax.axis_index("core") == 0
    depth = SUB // 2
    keep_ref[...] = jnp.where(first, total[:depth], total[depth:])
    send_ref[...] = jnp.where(first, total[depth:], total[:depth])


def join_kernel(keep_ref, got_ref, grad_ref):
    first = lax.axis_index("core") == 0
    keep, got = keep_ref[...], got_ref[...]
    grad_ref[:, 0, :] = jnp.where(first, keep, got)
    grad_ref[:, 1, :] = jnp.where(first, got, keep)


def per_device(inputs, doc_start, gate_weight, gate_bias, decay_rate, cotangent):
    _, rows, width = inputs.shape
    head_dim, heads, wide = gate_weight.shape
    n_x, n_z = lax.axis_size("x"), lax.axis_size("z")
    chips = n_x * n_z
    half = width // 2
    depth = SUB // 2
    shape = jax.ShapeDtypeStruct
    vmem = pl.BlockSpec(memory_space=pltpu.VMEM)

    def call(kernel, operands, outs, name, scratch=()):
        return pl.pallas_call(
            kernel,
            out_shape=outs,
            in_specs=[vmem] * len(operands),
            scratch_shapes=scratch,
            compiler_params=pltpu.CompilerParams(vmem_limit_bytes=16 << 20),
            name=name,
        )(*operands)

    swap = lambda value: lax.ppermute(value, "core", [(0, 1), (1, 0)])
    packed = shape((2 * rows + SUB, half), F32)
    gates = (jnp.moveaxis(gate_weight, 1, 0), gate_bias, decay_rate.reshape(1, width))
    operands = (inputs.reshape(rows, width), cotangent.reshape(rows, width), doc_start, gates[0])
    send, own = call(pack_kernel, operands, [packed] * 2, "pack")
    got = swap(send)
    fields = [shape((rows, half), BF16)] + [shape((rows, half), F32)] * 8
    tiles = half // LANES
    summary, *own = call(own_kernel, (own, *gates), [shape((3, tiles, LANES), F32)] + fields, "own_scans")
    spread, *got = call(
        got_kernel,
        (got, *gates, summary),
        [shape((chips, 3, 2 * tiles, LANES), F32)] + fields,
        "got_scans",
        [pltpu.VMEM((3, 2 * tiles, LANES), F32)],
    )
    everyone = lax.all_to_all(spread, ("x", "z"), 0, 0)
    out, states, dpre, direct, gw = call(
        lambda *refs: finish_kernel(n_x, n_z, *refs),
        (everyone, *own, *got),
        [
            shape((rows, half), BF16),
            shape((rows, half), F32),
            shape((2 * rows, wide), BF16),
            shape((2 * rows, half), F32),
            shape((chips, SUB, wide), F32),
        ],
        "finish",
    )
    pieces = lax.all_to_all(gw, ("x", "z"), 0, 0)
    gx, send = call(
        inputs_kernel, (dpre, direct, gates[0], states), [shape((rows, half), BF16), shape((2 * rows, half), F32)], "grad_inputs"
    )
    outputs, grad_inputs, order = call(
        unswap_kernel, (out, gx, swap(send)), [shape((rows, width), BF16)] * 2 + [shape((SUB, LANES), F32)], "unswap"
    )
    keep, give = call(sum_kernel, (pieces, order), [shape((depth, wide), F32)] * 2, "sum")
    grad_gate_weight = call(join_kernel, (keep, swap(give)), shape((depth, heads, wide), F32), "join")
    return (outputs[None], grad_inputs[None], grad_gate_weight)


def solution(mesh):
    n_dp, n_ctx, n_mp = mesh.devices.shape
    fine = Mesh(mesh.devices.reshape(n_dp // 2, 2, n_ctx, n_mp), ("x", "core", "z", "mp"))
    place = ("x", "core", "z")
    return jax.shard_map(
        per_device,
        mesh=fine,
        in_specs=(P(None, place, "mp"), P(None, place), P(None, "mp", None), P("mp", None), P("mp"), P(None, place, "mp")),
        out_specs=(P(None, place, "mp"), P(None, place, "mp"), P(place, "mp", None)),
        check_vma=False,
    )
```

time: 59 us -> 52.9 us (0.90)
  the two profiles are of different devices: /device:TPU:56 before, /device:TPU:1 now
where the time goes in v1:
time: 52.9 us; the launch traced here: 52.6 us
  blocking collectives  18.5 us (35%)
  starting transfers between devices  15 us (28%)
  waiting for transfers between devices  12.5 us (24%)
  Pallas kernels  4.09 us (8%)
  local copies, waits for them, and re-layouts  1.79 us (3%)
  between operations  0.72 us (1%)
    all_to_all x1, blocking collectives, per_device(): everyone = lax.all_to_all(spread, ('x', 'z'), 0, 0)  18.5 us
    all_to_all x1, waiting for transfers between devices, per_device(): pieces = lax.all_to_all(gw, ('x', 'z'), 0, 0)  9.92 us
    ppermute x3, starting transfers between devices, per_device(): swap = lambda value: lax.ppermute(value, 'core', [(0, 1), (1, 0)])  9.54 us
    all_to_all x1, starting transfers between devices, per_device(): pieces = lax.all_to_all(gw, ('x', 'z'), 0, 0)  5.46 us
    pallas_call x8, Pallas kernels, call(): pl.pallas_call(kernel, out_shape=outs, in_specs=[vmem] * len(operands), s...  4.09 us
    ppermute x3, waiting for transfers between devices, per_device(): swap = lambda value: lax.ppermute(value, 'core', [(0, 1), (1, 0)])  2.59 us
    unnamed x11, local copies, waits for them, and re-layouts  1.79 us
  transfers between devices with their start and end apart: 4, of which 4 were waited for; matrix products, arithmetic and copies ran while one was open for 0% of the time, Pallas kernels for 3%

profile of v1, /device:TPU:1, one launch (start us, length us, event | category | flops | bytes accessed | tf_op | source)
XLA Modules:
  0.0 52.6 jit_solution(16813634324951374715)
XLA Ops:
  0.6 0.0 copy-start.1
  0.6 0.0 copy-start
  0.7 1.1 %copy.11 = bf16[256,2,512]{2,0,1:T(8,128)(2,1)S(1)} copy(bf16[256,2,512]{2,1,0:T(2,128)(2,1)} %param.8) | data formatting | bytes 1048576 | tf_op args[2]
  1.8 0.0 copy-start.4
  1.8 0.0 copy-done.1
  1.8 0.0 copy-done
  1.8 0.6 %copy-done.4 = s32[1,128]{1,0:T(1,128)S(1)} copy-done((s32[1,128]{1,0:T(1,128)S(1)}, s32[1,128]{1,0:T(1,128)}, u32[]{:S(2)}) %copy-start.4) | copy-done | bytes 536
  2.4 0.0 copy-start.3
  2.5 0.1 pack.1
  2.5 0.0 copy-start.2
  2.5 3.3 %collective-permute-start = (f32[264,256]{1,0:T(8,128)S(1)}, f32[264,256]{1,0:T(8,128)S(1)}, u32[]{:S(2)}, u32[]{:S(2)}) collective-permute-start(f32[264,256]{1,0:T(8,128)S(1)} %get-tuple-element.37), channel_id=1, source_target_pairs={{0,32},{32,0},{1,33},{33,1},{2,34},{34,2},{3,35},{35,3},{4,36},{36... | collective-permute-start | bytes 811016 | tf_op jit(solution)/shard_map/ppermute | solution.py:245
  5.9 0.0 copy-done.3
  5.9 0.0 copy-done.2
  5.9 0.6 %own_scans.1 = (f32[3,2,128]{2,1,0:T(2,128)S(1)}, bf16[128,256]{1,0:T(8,128)(2,1)S(1)}, f32[128,256]{1,0:T(8,128)S(1)}, f32[128,256]{1,0:T(8,128)S(1)}, f32[128,...) custom-call(f32[264,256]{1,0:T(8,128)S(1)} %get-tuple-element.38.pac, ...), custom_call_target="tpu_custom_call" | custom-call | tf_op jit(solution)/shard_map/own_scans/pallas_call | solution.py:236
  6.4 0.6 %collective-permute-done.pack_ref = f32[264,256]{1,0:T(8,128)S(1)} collective-permute-done((f32[264,256]{1,0:T(8,128)S(1)}, f32[264,256]{1,0:T(8,128)S(1)}, u32[]{:S(2)}, u32[]{:S(2)}) %collective-permute-start) | collective-permute-done | bytes 270368 | tf_op jit(solution)/shard_map/ppermute | solution.py:245
  7.0 0.6 %got_scans.1 = (f32[32,3,4,128]{3,2,1,0:T(4,128)S(1)}, bf16[128,256]{1,0:T(8,128)(2,1)S(1)}, f32[128,256]{1,0:T(8,128)S(1)}, f32[128,256]{1,0:T(8,128)S(1)}, f32...) custom-call(f32[264,256]{1,0:T(8,128)S(1)} %collective-permute-done., ...), custom_call_target="tpu_custom_call" | custom-call | tf_op jit(solution)/shard_map/got_scans/pallas_call | solution.py:236
  7.6 18.5 %all_to_all.10.refs_0_ = f32[32,3,4,128]{3,2,1,0:T(4,128)S(1)} all-to-all(f32[32,3,4,128]{3,2,1,0:T(4,128)S(1)} %get-tuple-element.40), channel_id=1, replica_groups=mesh['x'=4,'core'=2,'z'=8,'mp'=4] {'x','z'}, dimensions={0} | all-to-all | bytes 393216 | tf_op jit(solution)/shard_map/all_to_all | solution.py:261
  26.1 1.2 %finish.1 = (bf16[128,256]{1,0:T(8,128)(2,1)S(1)}, f32[128,256]{1,0:T(8,128)S(1)}, bf16[256,512]{1,0:T(8,128)(2,1)S(1)}, f32[256,256]{1,0:T(8,128)S(1)}, f32[32,8,512]{2,1,0:T(8,128)}) custom-call(f32[32,3,4,128]{3,2,1,0:T(4,128)S(1)} %all_to_all.10.refs_0_, bf16[128,256]{1,0:T(8,128)(2,1)S(1)} %get-tuple-element.41.refs_1_, ...), custom_call_target="tpu_custom_call" | custom-call | tf_op jit(solution)/shard_map/finish/pallas_call | solution.py:236
  27.3 5.5 %all-to-all-start.1 = ((f32[32,8,512]{2,1,0:T(8,128)}), f32[32,8,512]{2,1,0:T(8,128)S(1)}, u32[]{:S(2)}, u32[]{:S(2)}) async-start(f32[32,8,512]{2,1,0:T(8,128)} %get-tuple-element.67), calls=%async_computation.1 | async-start | bytes 1048576 | tf_op jit(solution)/shard_map/all_to_all | solution.py:274
  32.8 0.3 grad_inputs.1
  33.1 1.6 %collective-permute-start.1 = (f32[256,256]{1,0:T(8,128)S(1)}, f32[256,256]{1,0:T(8,128)S(1)}, u32[]{:S(2)}, u32[]{:S(2)}) collective-permute-start(f32[256,256]{1,0:T(8,128)S(1)} %get-tuple-element.64), channel_id=1, source_target_pairs={{0,32},{32,0},{1,33},{33,1},{2,34},{34,2},{3,35},{35,3},{4,36},{36... | collective-permute-start | bytes 786440 | tf_op jit(solution)/shard_map/ppermute | solution.py:245
  34.7 1.2 %collective-permute-done.1.got_ref = f32[256,256]{1,0:T(8,128)S(1)} collective-permute-done((f32[256,256]{1,0:T(8,128)S(1)}, f32[256,256]{1,0:T(8,128)S(1)}, u32[]{:S(2)}, u32[]{:S(2)}) %collective-permute-start.1) | collective-permute-done | bytes 262176 | tf_op jit(solution)/shard_map/ppermute | solution.py:245
  35.9 0.7 %unswap.1 = (bf16[128,512]{1,0:T(8,128)(2,1)}, bf16[128,512]{1,0:T(8,128)(2,1)}, f32[8,128]{1,0:T(8,128)S(1)}) custom-call(bf16[128,256]{1,0:T(8,128)(2,1)S(1)} %get-tuple-element.59.out_ref, bf16[128,256]{1,0:T(8,128)(2,1)S(1)} %get-tuple-element.63.gx_ref, f32[256,256]{1,0:T(8,128)S(1)} %collective-permute-done.1.got_ref), custom_call_target="tpu_custom_call" | custom-call | tf_op jit(solution)/shard_map/unswap/pallas_call | solution.py:236
  36.6 9.9 %all-to-all-done.1.pieces_ref = f32[32,8,512]{2,1,0:T(8,128)S(1)} async-done(((f32[32,8,512]{2,1,0:T(8,128)}), f32[32,8,512]{2,1,0:T(8,128)S(1)}, u32[]{:S(2)}, u32[]{:S(2)}) %all-to-all-start.1) | async-done | bytes 524320 | tf_op jit(solution)/shard_map/all_to_all | solution.py:274
  46.6 4.6 %collective-permute-start.2 = (f32[4,512]{1,0:T(4,128)S(1)}, f32[4,512]{1,0:T(4,128)S(1)}, u32[]{:S(2)}, u32[]{:S(2)}) collective-permute-start(f32[4,512]{1,0:T(4,128)S(1)} %get-tuple-element.70), channel_id=1, source_target_pairs={{0,32},{32,0},{1,33},{33,1},{2,34},{34,2},{3,35},{35,3},{4,36},{36... | collective-permute-start | bytes 24584 | tf_op jit(solution)/shard_map/ppermute | solution.py:245
  51.2 0.8 %collective-permute-done.2.got_ref = f32[4,512]{1,0:T(4,128)S(1)} collective-permute-done((f32[4,512]{1,0:T(4,128)S(1)}, f32[4,512]{1,0:T(4,128)S(1)}, u32[]{:S(2)}, u32[]{:S(2)}) %collective-permute-start.2) | collective-permute-done | bytes 8224 | tf_op jit(solution)/shard_map/ppermute | solution.py:245
  52.0 0.6 %join.1 = f32[4,2,512]{2,1,0:T(2,128)} custom-call(f32[4,512]{1,0:T(4,128)S(1)} %get-tuple-element.69.keep_ref, f32[4,512]{1,0:T(4,128)S(1)} %collective-permute-done.2.got_ref), custom_call_target="tpu_custom_call" | custom-call | tf_op jit(solution)/shard_map/join/pallas_call | solution.py:236
  (1 shorter events, 0.0 us)
Async XLA Ops:
  0.6 1.2 %copy-start.1 = (bf16[1,128,512]{2,1,0:T(8,128)(2,1)S(1)}, bf16[1,128,512]{2,1,0:T(8,128)(2,1)}, u32[]{:S(2)}) copy-start(bf16[1,128,512]{2,1,0:T(8,128)(2,1)} %param.11) | copy-start | bytes 393220
  0.6 1.2 %copy-start = (bf16[1,128,512]{2,1,0:T(8,128)(2,1)S(1)}, bf16[1,128,512]{2,1,0:T(8,128)(2,1)}, u32[]{:S(2)}) copy-start(bf16[1,128,512]{2,1,0:T(8,128)(2,1)} %param.6) | copy-start | bytes 393220
  1.8 0.7 %copy-start.4 = (s32[1,128]{1,0:T(1,128)S(1)}, s32[1,128]{1,0:T(1,128)}, u32[]{:S(2)}) copy-start(s32[1,128]{1,0:T(1,128)} %doc_ref.1) | copy-start | bytes 1540
  2.4 3.4 %copy-start.3 = (f32[512]{0:T(512)S(1)}, f32[512]{0:T(512)}, u32[]{:S(2)}) copy-start(f32[512]{0:T(512)} %param.10) | copy-start | bytes 6148
  2.5 3.3 %copy-start.2 = (f32[2,512]{1,0:T(2,128)S(1)}, f32[2,512]{1,0:T(2,128)}, u32[]{:S(2)}) copy-start(f32[2,512]{1,0:T(2,128)} %bias_ref.3) | copy-start | bytes 12292
  2.5 4.5 %collective-permute-start = (f32[264,256]{1,0:T(8,128)S(1)}, f32[264,256]{1,0:T(8,128)S(1)}, u32[]{:S(2)}, u32[]{:S(2)}) collective-permute-start(f32[264,256]{1,0:T(8,128)S(1)} %get-tuple-element.37), channel_id=1, source_target_pairs={{0,32},{32,0},{1,33},{33,1},{2,34},{34,2},{3,35},{35,3},{4,36},{36... | collective-permute-start | bytes 811016 | tf_op jit(solution)/shard_map/ppermute | solution.py:245
  27.3 19.2 %all-to-all-start.1 = ((f32[32,8,512]{2,1,0:T(8,128)}), f32[32,8,512]{2,1,0:T(8,128)S(1)}, u32[]{:S(2)}, u32[]{:S(2)}) async-start(f32[32,8,512]{2,1,0:T(8,128)} %get-tuple-element.67), calls=%async_computation.1 | async-start | bytes 1048576 | tf_op jit(solution)/shard_map/all_to_all | solution.py:274
  33.1 2.8 %collective-permute-start.1 = (f32[256,256]{1,0:T(8,128)S(1)}, f32[256,256]{1,0:T(8,128)S(1)}, u32[]{:S(2)}, u32[]{:S(2)}) collective-permute-start(f32[256,256]{1,0:T(8,128)S(1)} %get-tuple-element.64), channel_id=1, source_target_pairs={{0,32},{32,0},{1,33},{33,1},{2,34},{34,2},{3,35},{35,3},{4,36},{36... | collective-permute-start | bytes 786440 | tf_op jit(solution)/shard_map/ppermute | solution.py:245
  46.6 5.4 %collective-permute-start.2 = (f32[4,512]{1,0:T(4,128)S(1)}, f32[4,512]{1,0:T(4,128)S(1)}, u32[]{:S(2)}, u32[]{:S(2)}) collective-permute-start(f32[4,512]{1,0:T(4,128)S(1)} %get-tuple-element.70), channel_id=1, source_target_pairs={{0,32},{32,0},{1,33},{33,1},{2,34},{34,2},{3,35},{35,3},{4,36},{36... | collective-permute-start | bytes 24584 | tf_op jit(solution)/shard_map/ppermute | solution.py:245

commit v2 on v1

--- a/solution.py
+++ b/solution.py
@@ -41,7 +41,11 @@
     return jnp.concatenate(a_out, 0), jnp.concatenate(b_out, 0), a_in, b_in
 
 
-def pack_kernel(x_ref, cot_ref, doc_ref, _, send_ref, own_ref):
+def head_kernel(order_ref):
+    order_ref[...] = jnp.zeros_like(order_ref)
+
+
+def pack_kernel(x_ref, cot_ref, doc_ref, bias_ref, rate_ref, order_ref, send_ref, own_ref):
     rows, width = x_ref.shape
     half = width // 2
     first = lax.axis_index("core") == 0
@@ -101,14 +105,16 @@
             summary_ref[i, part : part + 1, :] = value
 
 
-def got_kernel(pack_ref, w_ref, bias_ref, rate_ref, own_ref, spread_ref, *refs):
-    *refs, summary_ref = refs
+def got_kernel(pack_ref, w_ref, bias_ref, rate_ref, own_ref, summary_ref, *refs):
     core = lax.axis_index("core")
     ends = local_scans(pack_ref, w_ref, bias_ref, rate_ref, *refs)
     for part, values in enumerate(ends):
         for i, value in enumerate(values):
             summary_ref[i, pl.ds(core * len(ends) + part, 1), :] = own_ref[i, part : part + 1, :]
             summary_ref[i, pl.ds((1 - core) * len(ends) + part, 1), :] = value
+
+
+def spread_kernel(summary_ref, _, spread_ref):
     summary = summary_ref[...]
     for j in range(spread_ref.shape[0]):
         spread_ref[j] = summary
@@ -232,32 +238,31 @@
     shape = jax.ShapeDtypeStruct
     vmem = pl.BlockSpec(memory_space=pltpu.VMEM)
 
-    def call(kernel, operands, outs, name, scratch=()):
+    def call(kernel, operands, outs, name, scratch=(), cost=None):
         return pl.pallas_call(
             kernel,
             out_shape=outs,
             in_specs=[vmem] * len(operands),
             scratch_shapes=scratch,
             compiler_params=pltpu.CompilerParams(vmem_limit_bytes=16 << 20),
+            cost_estimate=cost,
             name=name,
         )(*operands)
 
     swap = lambda value: lax.ppermute(value, "core", [(0, 1), (1, 0)])
     packed = shape((2 * rows + SUB, half), F32)
     gates = (jnp.moveaxis(gate_weight, 1, 0), gate_bias, decay_rate.reshape(1, width))
-    operands = (inputs.reshape(rows, width), cotangent.reshape(rows, width), doc_start, gates[0])
+    cost = pl.CostEstimate(flops=4 * 10**9, bytes_accessed=4096, transcendentals=0)
+    order = call(head_kernel, (), shape((SUB, LANES), F32), "head", cost=cost)
+    operands = (inputs.reshape(rows, width), cotangent.reshape(rows, width), doc_start, *gates[1:], order)
     send, own = call(pack_kernel, operands, [packed] * 2, "pack")
     got = swap(send)
     fields = [shape((rows, half), BF16)] + [shape((rows, half), F32)] * 8
     tiles = half // LANES
     summary, *own = call(own_kernel, (own, *gates), [shape((3, tiles, LANES), F32)] + fields, "own_scans")
-    spread, *got = call(
-        got_kernel,
-        (got, *gates, summary),
-        [shape((chips, 3, 2 * tiles, LANES), F32)] + fields,
-        "got_scans",
-        [pltpu.VMEM((3, 2 * tiles, LANES), F32)],
-    )
+    summary, *got = call(got_kernel, (got, *gates, summary), [shape((3, 2 * tiles, LANES), F32)] + fields, "got_scans")
+    met = lax.ppermute(order, "z", [(i, i ^ 1) for i in range(n_z)])
+    spread = call(spread_kernel, (summary, met), shape((chips, 3, 2 * tiles, LANES), F32), "spread")
     everyone = lax.all_to_all(spread, ("x", "z"), 0, 0)
     out, states, dpre, direct, gw = call(
         lambda *refs: finish_kernel(n_x, n_z, *refs),

time: 52.9 us -> 51.3 us (0.970)
  waiting for transfers between devices: 12.5 us -> 10.9 us
  starting transfers between devices: 15 us -> 15.9 us
  local copies, waits for them, and re-layouts: 1.79 us -> 0.99 us
    all_to_all x1, waiting for transfers between devices: 9.92 us -> 7.63 us  [per_device(): pieces = lax.all_to_all(gw, ('x', 'z'), 0, 0)]
    ppermute x3, starting transfers between devices: 9.54 us -> 11.3 us  [per_device(): swap = lambda value: lax.ppermute(value, 'core', [(0, 1), (1, 0)])]
    all_to_all x1, starting transfers between devices: 5.46 us -> 4.53 us  [per_device(): pieces = lax.all_to_all(gw, ('x', 'z'), 0, 0)]
    unnamed x11 -> x13, local copies, waits for them, and re-layouts: 1.79 us -> 0.99 us
    ppermute x0 -> x1, waiting for transfers between devices: none -> 0.73 us  [per_device(): met = lax.ppermute(order, 'z', [(i, i ^ 1) for i in range(n_z)])]
    pallas_call x8 -> x10, Pallas kernels: 4.09 us -> 4.12 us  [call(): pl.pallas_call(kernel, out_shape=outs, in_specs=[vmem] * len(operands), s...]
  transfers between devices with their start and end apart: 4 -> 5, of which waited for: 4 -> 5; matrix products, arithmetic and copies ran while one was open for 0% -> 0% of each run, Pallas kernels for 3% -> 4%
where the time goes in v2:
time: 51.3 us; the launch traced here: 51.1 us
  blocking collectives  18.5 us (36%)
  starting transfers between devices  15.9 us (31%)
  waiting for transfers between devices  10.9 us (21%)
  Pallas kernels  4.12 us (8%)
  local copies, waits for them, and re-layouts  0.99 us (2%)
  between operations  0.74 us (1%)
    all_to_all x1, blocking collectives, per_device(): everyone = lax.all_to_all(spread, ('x', 'z'), 0, 0)  18.5 us
    ppermute x3, starting transfers between devices, per_device(): swap = lambda value: lax.ppermute(value, 'core', [(0, 1), (1, 0)])  11.3 us
    all_to_all x1, waiting for transfers between devices, per_device(): pieces = lax.all_to_all(gw, ('x', 'z'), 0, 0)  7.63 us
    all_to_all x1, starting transfers between devices, per_device(): pieces = lax.all_to_all(gw, ('x', 'z'), 0, 0)  4.53 us
    pallas_call x10, Pallas kernels, call(): pl.pallas_call(kernel, out_shape=outs, in_specs=[vmem] * len(operands), s...  4.12 us
    ppermute x3, waiting for transfers between devices, per_device(): swap = lambda value: lax.ppermute(value, 'core', [(0, 1), (1, 0)])  2.52 us
  transfers between devices with their start and end apart: 5, of which 5 were waited for; matrix products, arithmetic and copies ran while one was open for 0% of the time, Pallas kernels for 4%

profile of v2, /device:TPU:1, one launch (start us, length us, event | category | flops | bytes accessed | tf_op | source)
XLA Modules:
  0.0 51.1 jit_solution(9479882003636997778)
XLA Ops:
  0.6 0.0 copy-start.1
  0.6 0.0 copy-start
  0.7 0.0 copy-start.3
  0.7 0.0 copy-start.5
  0.7 0.0 copy-start.2
  0.7 0.0 copy-start.4
  0.7 0.8 %copy-done.1 = bf16[1,128,512]{2,1,0:T(8,128)(2,1)S(1)} copy-done((bf16[1,128,512]{2,1,0:T(8,128)(2,1)S(1)}, bf16[1,128,512]{2,1,0:T(8,128)(2,1)}, u32[]{:S(2)}) %copy-start.1) | copy-done | bytes 131096
  1.5 0.1 copy-done
  1.6 0.0 copy-done.3
  1.6 0.0 copy-done.2
  1.6 0.0 copy-done.4
  1.6 0.1 pack.1
  1.7 3.3 %collective-permute-start = (f32[264,256]{1,0:T(8,128)S(1)}, f32[264,256]{1,0:T(8,128)S(1)}, u32[]{:S(2)}, u32[]{:S(2)}) collective-permute-start(f32[264,256]{1,0:T(8,128)S(1)} %get-tuple-element.37), channel_id=1, source_target_pairs={{0,32},{32,0},{1,33},{33,1},{2,34},{34,2},{3,35},{35,3},{4,36},{36... | collective-permute-start | bytes 811016 | tf_op jit(solution)/shard_map/ppermute | solution.py:252
  5.0 0.0 collective-permute-start.1
  5.0 0.0 copy-done.5
  5.0 0.1 copy.11
  5.1 0.6 %own_scans.1 = (f32[3,2,128]{2,1,0:T(2,128)S(1)}, bf16[128,256]{1,0:T(8,128)(2,1)S(1)}, f32[128,256]{1,0:T(8,128)S(1)}, f32[128,256]{1,0:T(8,128)S(1)}, f32[128,...) custom-call(f32[264,256]{1,0:T(8,128)S(1)} %get-tuple-element.38.pac, ...), custom_call_target="tpu_custom_call" | custom-call | tf_op jit(solution)/shard_map/own_scans/pallas_call | solution.py:242
  5.7 0.5 %collective-permute-done.pack_ref = f32[264,256]{1,0:T(8,128)S(1)} collective-permute-done((f32[264,256]{1,0:T(8,128)S(1)}, f32[264,256]{1,0:T(8,128)S(1)}, u32[]{:S(2)}, u32[]{:S(2)}) %collective-permute-start) | collective-permute-done | bytes 270368 | tf_op jit(solution)/shard_map/ppermute | solution.py:252
  6.2 0.6 %got_scans.1 = (f32[3,4,128]{2,1,0:T(4,128)S(1)}, bf16[128,256]{1,0:T(8,128)(2,1)S(1)}, f32[128,256]{1,0:T(8,128)S(1)}, f32[128,256]{1,0:T(8,128)S(1)}, f32[128,...) custom-call(f32[264,256]{1,0:T(8,128)S(1)} %collective-permute-done., ...), custom_call_target="tpu_custom_call" | custom-call | tf_op jit(solution)/shard_map/got_scans/pallas_call | solution.py:242
  6.8 0.7 %collective-permute-done.1._ = f32[8,128]{1,0:T(8,128)S(1)} collective-permute-done((f32[8,128]{1,0:T(8,128)S(1)}, f32[8,128]{1,0:T(8,128)S(1)}, u32[]{:S(2)}, u32[]{:S(2)}) %collective-permute-start.1) | collective-permute-done | bytes 4128 | tf_op jit(solution)/shard_map/ppermute | solution.py:264
  7.5 18.5 %all_to_all.10.refs_0_ = f32[32,3,4,128]{3,2,1,0:T(4,128)S(1)} all-to-all(f32[32,3,4,128]{3,2,1,0:T(4,128)S(1)} %spread.1), channel_id=1, replica_groups=mesh['x'=4,'core'=2,'z'=8,'mp'=4] {'x','z'}, dimensions={0} | all-to-all | bytes 393216 | tf_op jit(solution)/shard_map/all_to_all | solution.py:266
  26.0 1.2 %finish.1 = (bf16[128,256]{1,0:T(8,128)(2,1)S(1)}, f32[128,256]{1,0:T(8,128)S(1)}, bf16[256,512]{1,0:T(8,128)(2,1)S(1)}, f32[256,256]{1,0:T(8,128)S(1)}, f32[32,8,512]{2,1,0:T(8,128)}) custom-call(f32[32,3,4,128]{3,2,1,0:T(4,128)S(1)} %all_to_all.10.refs_0_, bf16[128,256]{1,0:T(8,128)(2,1)S(1)} %get-tuple-element.41.refs_1_, ...), custom_call_target="tpu_custom_call" | custom-call | tf_op jit(solution)/shard_map/finish/pallas_call | solution.py:242
  27.2 4.5 %all-to-all-start.1 = ((f32[32,8,512]{2,1,0:T(8,128)}), f32[32,8,512]{2,1,0:T(8,128)S(1)}, u32[]{:S(2)}, u32[]{:S(2)}) async-start(f32[32,8,512]{2,1,0:T(8,128)} %get-tuple-element.67), calls=%async_computation.1 | async-start | bytes 1048576 | tf_op jit(solution)/shard_map/all_to_all | solution.py:279
  31.8 0.3 grad_inputs.1
  32.1 2.6 %collective-permute-start.2 = (f32[256,256]{1,0:T(8,128)S(1)}, f32[256,256]{1,0:T(8,128)S(1)}, u32[]{:S(2)}, u32[]{:S(2)}) collective-permute-start(f32[256,256]{1,0:T(8,128)S(1)} %get-tuple-element.64), channel_id=1, source_target_pairs={{0,32},{32,0},{1,33},{33,1},{2,34},{34,2},{3,35},{35,3},{4,36},{36... | collective-permute-start | bytes 786440 | tf_op jit(solution)/shard_map/ppermute | solution.py:252
  34.6 1.2 %collective-permute-done.2.got_ref = f32[256,256]{1,0:T(8,128)S(1)} collective-permute-done((f32[256,256]{1,0:T(8,128)S(1)}, f32[256,256]{1,0:T(8,128)S(1)}, u32[]{:S(2)}, u32[]{:S(2)}) %collective-permute-start.2) | collective-permute-done | bytes 262176 | tf_op jit(solution)/shard_map/ppermute | solution.py:252
  35.8 0.7 %unswap.1 = (bf16[128,512]{1,0:T(8,128)(2,1)}, bf16[128,512]{1,0:T(8,128)(2,1)}, f32[8,128]{1,0:T(8,128)S(1)}) custom-call(bf16[128,256]{1,0:T(8,128)(2,1)S(1)} %get-tuple-element.59.out_ref, bf16[128,256]{1,0:T(8,128)(2,1)S(1)} %get-tuple-element.63.gx_ref, f32[256,256]{1,0:T(8,128)S(1)} %collective-permute-done.2.got_ref), custom_call_target="tpu_custom_call" | custom-call | tf_op jit(solution)/shard_map/unswap/pallas_call | solution.py:242
  36.5 7.6 %all-to-all-done.1.pieces_ref = f32[32,8,512]{2,1,0:T(8,128)S(1)} async-done(((f32[32,8,512]{2,1,0:T(8,128)}), f32[32,8,512]{2,1,0:T(8,128)S(1)}, u32[]{:S(2)}, u32[]{:S(2)}) %all-to-all-start.1) | async-done | bytes 524320 | tf_op jit(solution)/shard_map/all_to_all | solution.py:279
  44.2 5.4 %collective-permute-start.3 = (f32[4,512]{1,0:T(4,128)S(1)}, f32[4,512]{1,0:T(4,128)S(1)}, u32[]{:S(2)}, u32[]{:S(2)}) collective-permute-start(f32[4,512]{1,0:T(4,128)S(1)} %get-tuple-element.70), channel_id=1, source_target_pairs={{0,32},{32,0},{1,33},{33,1},{2,34},{34,2},{3,35},{35,3},{4,36},{36... | collective-permute-start | bytes 24584 | tf_op jit(solution)/shard_map/ppermute | solution.py:252
  49.6 0.8 %collective-permute-done.3.got_ref = f32[4,512]{1,0:T(4,128)S(1)} collective-permute-done((f32[4,512]{1,0:T(4,128)S(1)}, f32[4,512]{1,0:T(4,128)S(1)}, u32[]{:S(2)}, u32[]{:S(2)}) %collective-permute-start.3) | collective-permute-done | bytes 8224 | tf_op jit(solution)/shard_map/ppermute | solution.py:252
  50.5 0.6 %join.1 = f32[4,2,512]{2,1,0:T(2,128)} custom-call(f32[4,512]{1,0:T(4,128)S(1)} %get-tuple-element.69.keep_ref, f32[4,512]{1,0:T(4,128)S(1)} %collective-permute-done.3.got_ref), custom_call_target="tpu_custom_call" | custom-call | tf_op jit(solution)/shard_map/join/pallas_call | solution.py:242
  (3 shorter events, 0.1 us)
Async XLA Ops:
  0.6 0.9 %copy-start.1 = (bf16[1,128,512]{2,1,0:T(8,128)(2,1)S(1)}, bf16[1,128,512]{2,1,0:T(8,128)(2,1)}, u32[]{:S(2)}) copy-start(bf16[1,128,512]{2,1,0:T(8,128)(2,1)} %param.11) | copy-start | bytes 393220
  0.6 1.0 %copy-start = (bf16[1,128,512]{2,1,0:T(8,128)(2,1)S(1)}, bf16[1,128,512]{2,1,0:T(8,128)(2,1)}, u32[]{:S(2)}) copy-start(bf16[1,128,512]{2,1,0:T(8,128)(2,1)} %param.6) | copy-start | bytes 393220
  0.7 1.0 %copy-start.3 = (f32[512]{0:T(512)S(1)}, f32[512]{0:T(512)}, u32[]{:S(2)}) copy-start(f32[512]{0:T(512)} %param.10) | copy-start | bytes 6148
  0.7 4.4 %copy-start.5 = (bf16[256,2,512]{2,1,0:T(2,128)(2,1)S(1)}, bf16[256,2,512]{2,1,0:T(2,128)(2,1)}, u32[]{:S(2)}) copy-start(bf16[256,2,512]{2,1,0:T(2,128)(2,1)} %param.8) | copy-start | bytes 1572868
  0.7 0.9 %copy-start.2 = (f32[2,512]{1,0:T(2,128)S(1)}, f32[2,512]{1,0:T(2,128)}, u32[]{:S(2)}) copy-start(f32[2,512]{1,0:T(2,128)} %bias_ref.5) | copy-start | bytes 12292
  0.7 0.9 %copy-start.4 = (s32[1,128]{1,0:T(1,128)S(1)}, s32[1,128]{1,0:T(1,128)}, u32[]{:S(2)}) copy-start(s32[1,128]{1,0:T(1,128)} %doc_ref.1) | copy-start | bytes 1540
  1.7 4.5 %collective-permute-start = (f32[264,256]{1,0:T(8,128)S(1)}, f32[264,256]{1,0:T(8,128)S(1)}, u32[]{:S(2)}, u32[]{:S(2)}) collective-permute-start(f32[264,256]{1,0:T(8,128)S(1)} %get-tuple-element.37), channel_id=1, source_target_pairs={{0,32},{32,0},{1,33},{33,1},{2,34},{34,2},{3,35},{35,3},{4,36},{36... | collective-permute-start | bytes 811016 | tf_op jit(solution)/shard_map/ppermute | solution.py:252
  5.0 2.5 %collective-permute-start.1 = (f32[8,128]{1,0:T(8,128)S(1)}, f32[8,128]{1,0:T(8,128)S(1)}, u32[]{:S(2)}, u32[]{:S(2)}) collective-permute-start(f32[8,128]{1,0:T(8,128)S(1)} %head.1.order_ref), channel_id=1, source_target_pairs={{0,4},{4,0},{8,12},{12,8},{16,20},{20,16},{24,28},{28,24},{1,5},{5... | collective-permute-start | bytes 12296 | tf_op jit(solution)/shard_map/ppermute | solution.py:264
  27.2 16.9 %all-to-all-start.1 = ((f32[32,8,512]{2,1,0:T(8,128)}), f32[32,8,512]{2,1,0:T(8,128)S(1)}, u32[]{:S(2)}, u32[]{:S(2)}) async-start(f32[32,8,512]{2,1,0:T(8,128)} %get-tuple-element.67), calls=%async_computation.1 | async-start | bytes 1048576 | tf_op jit(solution)/shard_map/all_to_all | solution.py:279
  32.1 3.7 %collective-permute-start.2 = (f32[256,256]{1,0:T(8,128)S(1)}, f32[256,256]{1,0:T(8,128)S(1)}, u32[]{:S(2)}, u32[]{:S(2)}) collective-permute-start(f32[256,256]{1,0:T(8,128)S(1)} %get-tuple-element.64), channel_id=1, source_target_pairs={{0,32},{32,0},{1,33},{33,1},{2,34},{34,2},{3,35},{35,3},{4,36},{36... | collective-permute-start | bytes 786440 | tf_op jit(solution)/shard_map/ppermute | solution.py:252
  44.2 6.3 %collective-permute-start.3 = (f32[4,512]{1,0:T(4,128)S(1)}, f32[4,512]{1,0:T(4,128)S(1)}, u32[]{:S(2)}, u32[]{:S(2)}) collective-permute-start(f32[4,512]{1,0:T(4,128)S(1)} %get-tuple-element.70), channel_id=1, source_target_pairs={{0,32},{32,0},{1,33},{33,1},{2,34},{34,2},{3,35},{35,3},{4,36},{36... | collective-permute-start | bytes 24584 | tf_op jit(solution)/shard_map/ppermute | solution.py:252

commit v3 on v1

--- a/solution.py
+++ b/solution.py
@@ -41,7 +41,11 @@
     return jnp.concatenate(a_out, 0), jnp.concatenate(b_out, 0), a_in, b_in
 
 
-def pack_kernel(x_ref, cot_ref, doc_ref, _, send_ref, own_ref):
+def head_kernel(order_ref):
+    order_ref[...] = jnp.zeros_like(order_ref)
+
+
+def pack_kernel(x_ref, cot_ref, doc_ref, bias_ref, rate_ref, order_ref, send_ref, own_ref):
     rows, width = x_ref.shape
     half = width // 2
     first = lax.axis_index("core") == 0
@@ -114,11 +118,11 @@
         spread_ref[j] = summary
 
 
-def fold(all_ref, order, kind, base, wanted=None):
+def fold(all_ref, order, kind, wanted=None):
     product = jnp.ones(all_ref.shape[2:], F32)
     value = jnp.zeros(all_ref.shape[2:], F32)
     for z in order:
-        a, b = all_ref[base + z, 0], all_ref[base + z, kind]
+        a, b = all_ref[z, 0], all_ref[z, kind]
         if wanted is not None:
             a, b = jnp.where(wanted(z), a, 1.0), jnp.where(wanted(z), b, 0.0)
         value = a * value + b
@@ -126,7 +130,14 @@
     return product, value
 
 
-def edges(all_ref, kind, x, z, n_x, n_z, backward):
+def totals_kernel(all_ref, totals_ref):
+    n_z = all_ref.shape[0]
+    totals_ref[0], totals_ref[1] = fold(all_ref, range(n_z), 1)
+    totals_ref[2] = fold(all_ref, range(n_z - 1, -1, -1), 2)[1]
+
+
+def edges(all_ref, rows, own, kind, x, z, backward):
+    n_x, n_z = len(rows), all_ref.shape[0]
     half = all_ref.shape[2] // 2
     cores = (slice(0, half), slice(half, 2 * half))
     near, far = (cores[1], cores[0]) if backward else cores
@@ -134,23 +145,29 @@
     apply = lambda link, at, value: link[0][at] * value + link[1][at]
     carried = jnp.zeros((half, LANES), F32)
     for i in range(n_x - 1, 0, -1) if backward else range(n_x - 1):
-        link = fold(all_ref, order, kind, i * n_z)
+        link = rows[i][0], rows[i][kind]
         carried = jnp.where(i > x if backward else i < x, apply(link, far, apply(link, near, carried)), carried)
-    base = x * n_z
-    whole = fold(all_ref, order, kind, base)
-    partial = fold(all_ref, order, kind, base, (lambda i: i > z) if backward else (lambda i: i < z))
+    partial = fold(all_ref, order, kind, (lambda i: i > z) if backward else (lambda i: i < z))
     ahead = apply(partial, near, carried)
-    behind = apply(partial, far, apply(whole, near, carried))
+    behind = apply(partial, far, apply((own[0], own[kind]), near, carried))
     return (behind, ahead) if backward else (ahead, behind)
 
 
 def finish_kernel(n_x, n_z, all_ref, *refs):
+    row_refs, refs = refs[:n_x], refs[n_x:]
     own, got, (out_ref, send_ref, dpre_ref, direct_ref, gw_ref) = refs[:9], refs[9:18], refs[18:]
     rows, half = out_ref.shape
     first = lax.axis_index("core") == 0
     at_x, at_z = lax.axis_index("x"), lax.axis_index("z")
-    entering = edges(all_ref, 1, at_x, at_z, n_x, n_z, False)
-    arriving = edges(all_ref, 2, at_x, at_z, n_x, n_z, True)
+    totals = [ref[...] for ref in row_refs]
+    ordered = []
+    for i in range(n_x):
+        here = totals[0]
+        for d in range(1, n_x):
+            here = jnp.where((at_x ^ d) == i, totals[d], here)
+        ordered.append(here)
+    entering = edges(all_ref, ordered, totals[0], 1, at_x, at_z, False)
+    arriving = edges(all_ref, ordered, totals[0], 2, at_x, at_z, True)
     row = lax.broadcasted_iota(jnp.int32, (rows, LANES), 0)
     weight_grad = 0.0
     for block, (x_ref, k1_ref, k2_ref, k3_ref, k4_ref, cum_ref, ls_ref, pc_ref, la_ref) in enumerate((own, got)):
@@ -232,20 +249,23 @@
     shape = jax.ShapeDtypeStruct
     vmem = pl.BlockSpec(memory_space=pltpu.VMEM)
 
-    def call(kernel, operands, outs, name, scratch=()):
+    def call(kernel, operands, outs, name, scratch=(), cost=None):
         return pl.pallas_call(
             kernel,
             out_shape=outs,
             in_specs=[vmem] * len(operands),
             scratch_shapes=scratch,
             compiler_params=pltpu.CompilerParams(vmem_limit_bytes=16 << 20),
+            cost_estimate=cost,
             name=name,
         )(*operands)
 
     swap = lambda value: lax.ppermute(value, "core", [(0, 1), (1, 0)])
     packed = shape((2 * rows + SUB, half), F32)
     gates = (jnp.moveaxis(gate_weight, 1, 0), gate_bias, decay_rate.reshape(1, width))
-    operands = (inputs.reshape(rows, width), cotangent.reshape(rows, width), doc_start, gates[0])
+    cost = pl.CostEstimate(flops=4 * 10**9, bytes_accessed=4096, transcendentals=0)
+    order = call(head_kernel, (), shape((SUB, LANES), F32), "head", cost=cost)
+    operands = (inputs.reshape(rows, width), cotangent.reshape(rows, width), doc_start, *gates[1:], order)
     send, own = call(pack_kernel, operands, [packed] * 2, "pack")
     got = swap(send)
     fields = [shape((rows, half), BF16)] + [shape((rows, half), F32)] * 8
@@ -254,14 +274,16 @@
     spread, *got = call(
         got_kernel,
         (got, *gates, summary),
-        [shape((chips, 3, 2 * tiles, LANES), F32)] + fields,
+        [shape((n_z, 3, 2 * tiles, LANES), F32)] + fields,
         "got_scans",
         [pltpu.VMEM((3, 2 * tiles, LANES), F32)],
     )
-    everyone = lax.all_to_all(spread, ("x", "z"), 0, 0)
+    row = lax.all_to_all(spread, "z", 0, 0)
+    totals = call(totals_kernel, (row,), shape((3, 2 * tiles, LANES), F32), "totals")
+    rows_x = [totals] + [lax.ppermute(totals, "x", [(i, i ^ d) for i in range(n_x)]) for d in range(1, n_x)]
     out, states, dpre, direct, gw = call(
         lambda *refs: finish_kernel(n_x, n_z, *refs),
-        (everyone, *own, *got),
+        (row, *rows_x, *own, *got),
         [
             shape((rows, half), BF16),
             shape((rows, half), F32),

time: 52.9 us -> 51.3 us (0.970)
  blocking collectives: 18.5 us -> 13.3 us
  starting transfers between devices: 15 us -> 19.5 us
  local copies, waits for them, and re-layouts: 1.79 us -> 0.99 us
    all_to_all x1, blocking collectives: 18.5 us -> 13.3 us  [per_device(): row = lax.all_to_all(spread, 'z', 0, 0)]
    ppermute x0 -> x3, starting transfers between devices: none -> 3.34 us  [per_device(): lax.ppermute(totals, 'x', [(i, i ^ d) for i in range(n_x)])]
    all_to_all x1, waiting for transfers between devices: 9.92 us -> 6.64 us  [per_device(): pieces = lax.all_to_all(gw, ('x', 'z'), 0, 0)]
    ppermute x0 -> x3, waiting for transfers between devices: none -> 3.21 us  [per_device(): lax.ppermute(totals, 'x', [(i, i ^ d) for i in range(n_x)])]
    ppermute x3, starting transfers between devices: 9.54 us -> 12.3 us  [per_device(): swap = lambda value: lax.ppermute(value, 'core', [(0, 1), (1, 0)])]
    all_to_all x1, starting transfers between devices: 5.46 us -> 3.89 us  [per_device(): pieces = lax.all_to_all(gw, ('x', 'z'), 0, 0)]
    unnamed x11 -> x13, local copies, waits for them, and re-layouts: 1.79 us -> 0.99 us
    pallas_call x8 -> x10, Pallas kernels: 4.09 us -> 4.1 us  [call(): pl.pallas_call(kernel, out_shape=outs, in_specs=[vmem] * len(operands), s...]
  transfers between devices with their start and end apart: 4 -> 7, of which waited for: 4 -> 6; matrix products, arithmetic and copies ran while one was open for 0% -> 0% of each run, Pallas kernels for 3% -> 3%
where the time goes in v3:
time: 51.3 us; the launch traced here: 51 us
  starting transfers between devices  19.5 us (38%)
  blocking collectives  13.3 us (26%)
  waiting for transfers between devices  12.4 us (24%)
  Pallas kernels  4.1 us (8%)
  local copies, waits for them, and re-layouts  0.99 us (2%)
  between operations  0.73 us (1%)
    all_to_all x1, blocking collectives, per_device(): row = lax.all_to_all(spread, 'z', 0, 0)  13.3 us
    ppermute x3, starting transfers between devices, per_device(): swap = lambda value: lax.ppermute(value, 'core', [(0, 1), (1, 0)])  12.3 us
    all_to_all x1, waiting for transfers between devices, per_device(): pieces = lax.all_to_all(gw, ('x', 'z'), 0, 0)  6.64 us
    pallas_call x10, Pallas kernels, call(): pl.pallas_call(kernel, out_shape=outs, in_specs=[vmem] * len(operands), s...  4.1 us
    all_to_all x1, starting transfers between devices, per_device(): pieces = lax.all_to_all(gw, ('x', 'z'), 0, 0)  3.89 us
    ppermute x3, starting transfers between devices, per_device(): lax.ppermute(totals, 'x', [(i, i ^ d) for i in range(n_x)])  3.34 us
    ppermute x3, waiting for transfers between devices, per_device(): lax.ppermute(totals, 'x', [(i, i ^ d) for i in range(n_x)])  3.21 us
    ppermute x3, waiting for transfers between devices, per_device(): swap = lambda value: lax.ppermute(value, 'core', [(0, 1), (1, 0)])  2.53 us
  transfers between devices with their start and end apart: 7, of which 6 were waited for; matrix products, arithmetic and copies ran while one was open for 0% of the time, Pallas kernels for 3%

profile of v3, /device:TPU:1, one launch (start us, length us, event | category | flops | bytes accessed | tf_op | source)
XLA Modules:
  0.0 51.0 jit_solution(7033128686497481243)
XLA Ops:
  0.6 0.0 copy-start.1
  0.6 0.0 copy-start
  0.7 0.0 copy-start.3
  0.7 0.0 copy-start.5
  0.7 0.0 copy-start.2
  0.7 0.0 copy-start.4
  0.7 0.8 %copy-done.1 = bf16[1,128,512]{2,1,0:T(8,128)(2,1)S(1)} copy-done((bf16[1,128,512]{2,1,0:T(8,128)(2,1)S(1)}, bf16[1,128,512]{2,1,0:T(8,128)(2,1)}, u32[]{:S(2)}) %copy-start.1) | copy-done | bytes 131096
  1.5 0.1 copy-done
  1.6 0.0 copy-done.3
  1.6 0.1 pack.1
  1.7 3.3 %collective-permute-start = (f32[264,256]{1,0:T(8,128)S(1)}, f32[264,256]{1,0:T(8,128)S(1)}, u32[]{:S(2)}, u32[]{:S(2)}) collective-permute-start(f32[264,256]{1,0:T(8,128)S(1)} %get-tuple-element.37), channel_id=1, source_target_pairs={{0,32},{32,0},{1,33},{33,1},{2,34},{34,2},{3,35},{35,3},{4,36},{36... | collective-permute-start | bytes 811016 | tf_op jit(solution)/shard_map/ppermute | solution.py:263
  5.0 0.1 copy.11
  5.1 0.6 %own_scans.1 = (f32[3,2,128]{2,1,0:T(2,128)S(1)}, bf16[128,256]{1,0:T(8,128)(2,1)S(1)}, f32[128,256]{1,0:T(8,128)S(1)}, f32[128,256]{1,0:T(8,128)S(1)}, f32[128,...) custom-call(f32[264,256]{1,0:T(8,128)S(1)} %get-tuple-element.38.pac, ...), custom_call_target="tpu_custom_call" | custom-call | tf_op jit(solution)/shard_map/own_scans/pallas_call | solution.py:253
  5.7 0.5 %collective-permute-done.pack_ref = f32[264,256]{1,0:T(8,128)S(1)} collective-permute-done((f32[264,256]{1,0:T(8,128)S(1)}, f32[264,256]{1,0:T(8,128)S(1)}, u32[]{:S(2)}, u32[]{:S(2)}) %collective-permute-start) | collective-permute-done | bytes 270368 | tf_op jit(solution)/shard_map/ppermute | solution.py:263
  6.2 0.6 %got_scans.1 = (f32[8,3,4,128]{3,2,1,0:T(4,128)S(1)}, bf16[128,256]{1,0:T(8,128)(2,1)S(1)}, f32[128,256]{1,0:T(8,128)S(1)}, f32[128,256]{1,0:T(8,128)S(1)}, f32[...) custom-call(f32[264,256]{1,0:T(8,128)S(1)} %collective-permute-done., ...), custom_call_target="tpu_custom_call" | custom-call | tf_op jit(solution)/shard_map/got_scans/pallas_call | solution.py:253
  6.8 13.3 %all_to_all.10.all_ref.refs_0_ = f32[8,3,4,128]{3,2,1,0:T(4,128)S(1)} all-to-all(f32[8,3,4,128]{3,2,1,0:T(4,128)S(1)} %get-tuple-element.40), channel_id=1, replica_groups=mesh['x'=4,'core'=2,'z'=8,'mp'=4] {'z'}, dimensions={0} | all-to-all | bytes 98304 | tf_op jit(solution)/shard_map/all_to_all | solution.py:281
  20.1 2.6 %collective-permute-start.3 = (f32[3,4,128]{2,1,0:T(4,128)S(1)}, f32[3,4,128]{2,1,0:T(4,128)S(1)}, u32[]{:S(2)}, u32[]{:S(2)}) collective-permute-start(f32[3,4,128]{2,1,0:T(4,128)S(1)} %totals.1.refs_1_), channel_id=1, source_target_pairs={{0,192},{64,128},{128,64},{192,0},{1,193},{65,129},{129,65},{193,1... | collective-permute-start | bytes 18440 | tf_op jit(solution)/shard_map/ppermute | solution.py:283
  22.7 0.5 %collective-permute-start.2 = (f32[3,4,128]{2,1,0:T(4,128)S(1)}, f32[3,4,128]{2,1,0:T(4,128)S(1)}, u32[]{:S(2)}, u32[]{:S(2)}) collective-permute-start(f32[3,4,128]{2,1,0:T(4,128)S(1)} %totals.1.refs_1_), channel_id=1, source_target_pairs={{0,128},{64,192},{128,0},{192,64},{1,129},{65,193},{129,1},{193,65... | collective-permute-start | bytes 18440 | tf_op jit(solution)/shard_map/ppermute | solution.py:283
  23.2 0.3 collective-permute-start.1
  23.4 0.4 collective-permute-done.3.refs_4_
  23.9 2.8 %collective-permute-done.2.refs_3_ = f32[3,4,128]{2,1,0:T(4,128)S(1)} collective-permute-done((f32[3,4,128]{2,1,0:T(4,128)S(1)}, f32[3,4,128]{2,1,0:T(4,128)S(1)}, u32[]{:S(2)}, u32[]{:S(2)}) %collective-permute-start.2) | collective-permute-done | bytes 6176 | tf_op jit(solution)/shard_map/ppermute | solution.py:283
  26.6 0.0 collective-permute-done.1.refs_2_
  26.6 1.2 %finish.1 = (bf16[128,256]{1,0:T(8,128)(2,1)S(1)}, f32[128,256]{1,0:T(8,128)S(1)}, bf16[256,512]{1,0:T(8,128)(2,1)S(1)}, f32[256,256]{1,0:T(8,128)S(1)}, f32[32,8,512]{2,1,0:T(8,128)}) custom-call(f32[8,3,4,128]{3,2,1,0:T(4,128)S(1)} %all_to_all.10.all_ref.refs_0_, f32[3,4,128]{2,1,0:T(4,128)S(1)} %totals.1.refs_1_, ...), custom_call_target="tpu_custom_call" | custom-call | tf_op jit(solution)/shard_map/finish/pallas_call | solution.py:253
  27.9 3.9 %all-to-all-start.1 = ((f32[32,8,512]{2,1,0:T(8,128)}), f32[32,8,512]{2,1,0:T(8,128)S(1)}, u32[]{:S(2)}, u32[]{:S(2)}) async-start(f32[32,8,512]{2,1,0:T(8,128)} %get-tuple-element.67), calls=%async_computation.1 | async-start | bytes 1048576 | tf_op jit(solution)/shard_map/all_to_all | solution.py:296
  31.8 0.3 grad_inputs.1
  32.0 3.3 %collective-permute-start.4 = (f32[256,256]{1,0:T(8,128)S(1)}, f32[256,256]{1,0:T(8,128)S(1)}, u32[]{:S(2)}, u32[]{:S(2)}) collective-permute-start(f32[256,256]{1,0:T(8,128)S(1)} %get-tuple-element.64), channel_id=1, source_target_pairs={{0,32},{32,0},{1,33},{33,1},{2,34},{34,2},{3,35},{35,3},{4,36},{36... | collective-permute-start | bytes 786440 | tf_op jit(solution)/shard_map/ppermute | solution.py:263
  35.4 1.2 %collective-permute-done.4.got_ref = f32[256,256]{1,0:T(8,128)S(1)} collective-permute-done((f32[256,256]{1,0:T(8,128)S(1)}, f32[256,256]{1,0:T(8,128)S(1)}, u32[]{:S(2)}, u32[]{:S(2)}) %collective-permute-start.4) | collective-permute-done | bytes 262176 | tf_op jit(solution)/shard_map/ppermute | solution.py:263
  36.5 0.7 %unswap.1 = (bf16[128,512]{1,0:T(8,128)(2,1)}, bf16[128,512]{1,0:T(8,128)(2,1)}, f32[8,128]{1,0:T(8,128)S(1)}) custom-call(bf16[128,256]{1,0:T(8,128)(2,1)S(1)} %get-tuple-element.59.out_ref, bf16[128,256]{1,0:T(8,128)(2,1)S(1)} %get-tuple-element.63.gx_ref, f32[256,256]{1,0:T(8,128)S(1)} %collective-permute-done.4.got_ref), custom_call_target="tpu_custom_call" | custom-call | tf_op jit(solution)/shard_map/unswap/pallas_call | solution.py:253
  37.3 6.6 %all-to-all-done.1.pieces_ref = f32[32,8,512]{2,1,0:T(8,128)S(1)} async-done(((f32[32,8,512]{2,1,0:T(8,128)}), f32[32,8,512]{2,1,0:T(8,128)S(1)}, u32[]{:S(2)}, u32[]{:S(2)}) %all-to-all-start.1) | async-done | bytes 524320 | tf_op jit(solution)/shard_map/all_to_all | solution.py:296
  43.9 5.6 %collective-permute-start.5 = (f32[4,512]{1,0:T(4,128)S(1)}, f32[4,512]{1,0:T(4,128)S(1)}, u32[]{:S(2)}, u32[]{:S(2)}) collective-permute-start(f32[4,512]{1,0:T(4,128)S(1)} %get-tuple-element.70), channel_id=1, source_target_pairs={{0,32},{32,0},{1,33},{33,1},{2,34},{34,2},{3,35},{35,3},{4,36},{36... | collective-permute-start | bytes 24584 | tf_op jit(solution)/shard_map/ppermute | solution.py:263
  49.6 0.8 %collective-permute-done.5.got_ref = f32[4,512]{1,0:T(4,128)S(1)} collective-permute-done((f32[4,512]{1,0:T(4,128)S(1)}, f32[4,512]{1,0:T(4,128)S(1)}, u32[]{:S(2)}, u32[]{:S(2)}) %collective-permute-start.5) | collective-permute-done | bytes 8224 | tf_op jit(solution)/shard_map/ppermute | solution.py:263
  50.4 0.6 %join.1 = f32[4,2,512]{2,1,0:T(2,128)} custom-call(f32[4,512]{1,0:T(4,128)S(1)} %get-tuple-element.69.keep_ref, f32[4,512]{1,0:T(4,128)S(1)} %collective-permute-done.5.got_ref), custom_call_target="tpu_custom_call" | custom-call | tf_op jit(solution)/shard_map/join/pallas_call | solution.py:253
  (6 shorter events, 0.1 us)
Async XLA Ops:
  0.6 0.9 %copy-start.1 = (bf16[1,128,512]{2,1,0:T(8,128)(2,1)S(1)}, bf16[1,128,512]{2,1,0:T(8,128)(2,1)}, u32[]{:S(2)}) copy-start(bf16[1,128,512]{2,1,0:T(8,128)(2,1)} %param.11) | copy-start | bytes 393220
  0.6 1.0 %copy-start = (bf16[1,128,512]{2,1,0:T(8,128)(2,1)S(1)}, bf16[1,128,512]{2,1,0:T(8,128)(2,1)}, u32[]{:S(2)}) copy-start(bf16[1,128,512]{2,1,0:T(8,128)(2,1)} %param.6) | copy-start | bytes 393220
  0.7 1.0 %copy-start.3 = (f32[512]{0:T(512)S(1)}, f32[512]{0:T(512)}, u32[]{:S(2)}) copy-start(f32[512]{0:T(512)} %param.10) | copy-start | bytes 6148
  0.7 4.4 %copy-start.5 = (bf16[256,2,512]{2,1,0:T(2,128)(2,1)S(1)}, bf16[256,2,512]{2,1,0:T(2,128)(2,1)}, u32[]{:S(2)}) copy-start(bf16[256,2,512]{2,1,0:T(2,128)(2,1)} %param.8) | copy-start | bytes 1572868
  0.7 0.9 %copy-start.2 = (f32[2,512]{1,0:T(2,128)S(1)}, f32[2,512]{1,0:T(2,128)}, u32[]{:S(2)}) copy-start(f32[2,512]{1,0:T(2,128)} %bias_ref.5) | copy-start | bytes 12292
  0.7 0.9 %copy-start.4 = (s32[1,128]{1,0:T(1,128)S(1)}, s32[1,128]{1,0:T(1,128)}, u32[]{:S(2)}) copy-start(s32[1,128]{1,0:T(1,128)} %doc_ref.1) | copy-start | bytes 1540
  1.7 4.5 %collective-permute-start = (f32[264,256]{1,0:T(8,128)S(1)}, f32[264,256]{1,0:T(8,128)S(1)}, u32[]{:S(2)}, u32[]{:S(2)}) collective-permute-start(f32[264,256]{1,0:T(8,128)S(1)} %get-tuple-element.37), channel_id=1, source_target_pairs={{0,32},{32,0},{1,33},{33,1},{2,34},{34,2},{3,35},{35,3},{4,36},{36... | collective-permute-start | bytes 811016 | tf_op jit(solution)/shard_map/ppermute | solution.py:263
  20.1 3.8 %collective-permute-start.3 = (f32[3,4,128]{2,1,0:T(4,128)S(1)}, f32[3,4,128]{2,1,0:T(4,128)S(1)}, u32[]{:S(2)}, u32[]{:S(2)}) collective-permute-start(f32[3,4,128]{2,1,0:T(4,128)S(1)} %totals.1.refs_1_), channel_id=1, source_target_pairs={{0,192},{64,128},{128,64},{192,0},{1,193},{65,129},{129,65},{193,1... | collective-permute-start | bytes 18440 | tf_op jit(solution)/shard_map/ppermute | solution.py:283
  22.7 4.0 %collective-permute-start.2 = (f32[3,4,128]{2,1,0:T(4,128)S(1)}, f32[3,4,128]{2,1,0:T(4,128)S(1)}, u32[]{:S(2)}, u32[]{:S(2)}) collective-permute-start(f32[3,4,128]{2,1,0:T(4,128)S(1)} %totals.1.refs_1_), channel_id=1, source_target_pairs={{0,128},{64,192},{128,0},{192,64},{1,129},{65,193},{129,1},{193,65... | collective-permute-start | bytes 18440 | tf_op jit(solution)/shard_map/ppermute | solution.py:283
  23.2 3.5 %collective-permute-start.1 = (f32[3,4,128]{2,1,0:T(4,128)S(1)}, f32[3,4,128]{2,1,0:T(4,128)S(1)}, u32[]{:S(2)}, u32[]{:S(2)}) collective-permute-start(f32[3,4,128]{2,1,0:T(4,128)S(1)} %totals.1.refs_1_), channel_id=1, source_target_pairs={{0,64},{64,0},{128,192},{192,128},{1,65},{65,1},{129,193},{193,129... | collective-permute-start | bytes 18440 | tf_op jit(solution)/shard_map/ppermute | solution.py:283
  27.9 16.0 %all-to-all-start.1 = ((f32[32,8,512]{2,1,0:T(8,128)}), f32[32,8,512]{2,1,0:T(8,128)S(1)}, u32[]{:S(2)}, u32[]{:S(2)}) async-start(f32[32,8,512]{2,1,0:T(8,128)} %get-tuple-element.67), calls=%async_computation.1 | async-start | bytes 1048576 | tf_op jit(solution)/shard_map/all_to_all | solution.py:296
  32.0 4.5 %collective-permute-start.4 = (f32[256,256]{1,0:T(8,128)S(1)}, f32[256,256]{1,0:T(8,128)S(1)}, u32[]{:S(2)}, u32[]{:S(2)}) collective-permute-start(f32[256,256]{1,0:T(8,128)S(1)} %get-tuple-element.64), channel_id=1, source_target_pairs={{0,32},{32,0},{1,33},{33,1},{2,34},{34,2},{3,35},{35,3},{4,36},{36... | collective-permute-start | bytes 786440 | tf_op jit(solution)/shard_map/ppermute | solution.py:263
  43.9 6.5 %collective-permute-start.5 = (f32[4,512]{1,0:T(4,128)S(1)}, f32[4,512]{1,0:T(4,128)S(1)}, u32[]{:S(2)}, u32[]{:S(2)}) collective-permute-start(f32[4,512]{1,0:T(4,128)S(1)} %get-tuple-element.70), channel_id=1, source_target_pairs={{0,32},{32,0},{1,33},{33,1},{2,34},{34,2},{3,35},{35,3},{4,36},{36... | collective-permute-start | bytes 24584 | tf_op jit(solution)/shard_map/ppermute | solution.py:263

commit v4 on v2

--- a/solution.py
+++ b/solution.py
@@ -78,9 +78,10 @@
         decay = jnp.exp(rate * rgate)
         carry = decay * keep
         square = decay * decay
-        root = jnp.sqrt(1.0 - square + 0.01)
-        scale = jnp.where(kept, root, 1.0)
-        dscale = jnp.where(kept, -square / root, 0.0)
+        floored = 1.0 - square + 0.01
+        inverse = lax.rsqrt(floored)
+        scale = jnp.where(kept, floored * inverse, 1.0)
+        dscale = jnp.where(kept, -square * inverse, 0.0)
         slope = rate * (rgate * (1.0 - rgate))
         k4 = scale * igate
         drive = k4 * x

time: 51.3 us -> 51.3 us (level)
  no operation moved by 1% of the time
where the time goes in v4:
time: 51.3 us; the launch traced here: 51.1 us
  blocking collectives  18.5 us (36%)
  starting transfers between devices  15.9 us (31%)
  waiting for transfers between devices  10.9 us (21%)
  Pallas kernels  4.07 us (8%)
  local copies, waits for them, and re-layouts  0.99 us (2%)
  between operations  0.73 us (1%)
    all_to_all x1, blocking collectives, per_device(): everyone = lax.all_to_all(spread, ('x', 'z'), 0, 0)  18.5 us
    ppermute x3, starting transfers between devices, per_device(): swap = lambda value: lax.ppermute(value, 'core', [(0, 1), (1, 0)])  11.3 us
    all_to_all x1, waiting for transfers between devices, per_device(): pieces = lax.all_to_all(gw, ('x', 'z'), 0, 0)  7.63 us
    all_to_all x1, starting transfers between devices, per_device(): pieces = lax.all_to_all(gw, ('x', 'z'), 0, 0)  4.53 us
    pallas_call x10, Pallas kernels, call(): pl.pallas_call(kernel, out_shape=outs, in_specs=[vmem] * len(operands), s...  4.07 us
    ppermute x3, waiting for transfers between devices, per_device(): swap = lambda value: lax.ppermute(value, 'core', [(0, 1), (1, 0)])  2.54 us
  transfers between devices with their start and end apart: 5, of which 5 were waited for; matrix products, arithmetic and copies ran while one was open for 0% of the time, Pallas kernels for 4%

profile of v4, /device:TPU:1, one launch (start us, length us, event | category | flops | bytes accessed | tf_op | source)
XLA Modules:
  0.0 51.1 jit_solution(12548279982957142095)
XLA Ops:
  0.6 0.0 copy-start.1
  0.6 0.0 copy-start
  0.7 0.0 copy-start.3
  0.7 0.0 copy-start.5
  0.7 0.0 copy-start.2
  0.7 0.0 copy-start.4
  0.7 0.8 %copy-done.1 = bf16[1,128,512]{2,1,0:T(8,128)(2,1)S(1)} copy-done((bf16[1,128,512]{2,1,0:T(8,128)(2,1)S(1)}, bf16[1,128,512]{2,1,0:T(8,128)(2,1)}, u32[]{:S(2)}) %copy-start.1) | copy-done | bytes 131096
  1.5 0.1 copy-done
  1.6 0.0 copy-done.3
  1.6 0.0 copy-done.2
  1.6 0.0 copy-done.4
  1.6 0.1 pack.1
  1.7 3.3 %collective-permute-start = (f32[264,256]{1,0:T(8,128)S(1)}, f32[264,256]{1,0:T(8,128)S(1)}, u32[]{:S(2)}, u32[]{:S(2)}) collective-permute-start(f32[264,256]{1,0:T(8,128)S(1)} %get-tuple-element.37), channel_id=1, source_target_pairs={{0,32},{32,0},{1,33},{33,1},{2,34},{34,2},{3,35},{35,3},{4,36},{36... | collective-permute-start | bytes 811016 | tf_op jit(solution)/shard_map/ppermute | solution.py:253
  5.0 0.0 collective-permute-start.1
  5.0 0.0 copy-done.5
  5.0 0.1 copy.11
  5.1 0.6 %own_scans.1 = (f32[3,2,128]{2,1,0:T(2,128)S(1)}, bf16[128,256]{1,0:T(8,128)(2,1)S(1)}, f32[128,256]{1,0:T(8,128)S(1)}, f32[128,256]{1,0:T(8,128)S(1)}, f32[128,...) custom-call(f32[264,256]{1,0:T(8,128)S(1)} %get-tuple-element.38.pac, ...), custom_call_target="tpu_custom_call" | custom-call | tf_op jit(solution)/shard_map/own_scans/pallas_call | solution.py:243
  5.6 0.6 %collective-permute-done.pack_ref = f32[264,256]{1,0:T(8,128)S(1)} collective-permute-done((f32[264,256]{1,0:T(8,128)S(1)}, f32[264,256]{1,0:T(8,128)S(1)}, u32[]{:S(2)}, u32[]{:S(2)}) %collective-permute-start) | collective-permute-done | bytes 270368 | tf_op jit(solution)/shard_map/ppermute | solution.py:253
  6.2 0.5 %got_scans.1 = (f32[3,4,128]{2,1,0:T(4,128)S(1)}, bf16[128,256]{1,0:T(8,128)(2,1)S(1)}, f32[128,256]{1,0:T(8,128)S(1)}, f32[128,256]{1,0:T(8,128)S(1)}, f32[128,...) custom-call(f32[264,256]{1,0:T(8,128)S(1)} %collective-permute-done., ...), custom_call_target="tpu_custom_call" | custom-call | tf_op jit(solution)/shard_map/got_scans/pallas_call | solution.py:243
  6.7 0.8 %collective-permute-done.1._ = f32[8,128]{1,0:T(8,128)S(1)} collective-permute-done((f32[8,128]{1,0:T(8,128)S(1)}, f32[8,128]{1,0:T(8,128)S(1)}, u32[]{:S(2)}, u32[]{:S(2)}) %collective-permute-start.1) | collective-permute-done | bytes 4128 | tf_op jit(solution)/shard_map/ppermute | solution.py:265
  7.5 18.5 %all_to_all.10.refs_0_ = f32[32,3,4,128]{3,2,1,0:T(4,128)S(1)} all-to-all(f32[32,3,4,128]{3,2,1,0:T(4,128)S(1)} %spread.1), channel_id=1, replica_groups=mesh['x'=4,'core'=2,'z'=8,'mp'=4] {'x','z'}, dimensions={0} | all-to-all | bytes 393216 | tf_op jit(solution)/shard_map/all_to_all | solution.py:267
  26.0 1.2 %finish.1 = (bf16[128,256]{1,0:T(8,128)(2,1)S(1)}, f32[128,256]{1,0:T(8,128)S(1)}, bf16[256,512]{1,0:T(8,128)(2,1)S(1)}, f32[256,256]{1,0:T(8,128)S(1)}, f32[32,8,512]{2,1,0:T(8,128)}) custom-call(f32[32,3,4,128]{3,2,1,0:T(4,128)S(1)} %all_to_all.10.refs_0_, bf16[128,256]{1,0:T(8,128)(2,1)S(1)} %get-tuple-element.41.refs_1_, ...), custom_call_target="tpu_custom_call" | custom-call | tf_op jit(solution)/shard_map/finish/pallas_call | solution.py:243
  27.2 4.5 %all-to-all-start.1 = ((f32[32,8,512]{2,1,0:T(8,128)}), f32[32,8,512]{2,1,0:T(8,128)S(1)}, u32[]{:S(2)}, u32[]{:S(2)}) async-start(f32[32,8,512]{2,1,0:T(8,128)} %get-tuple-element.67), calls=%async_computation.1 | async-start | bytes 1048576 | tf_op jit(solution)/shard_map/all_to_all | solution.py:280
  31.8 0.3 grad_inputs.1
  32.1 2.6 %collective-permute-start.2 = (f32[256,256]{1,0:T(8,128)S(1)}, f32[256,256]{1,0:T(8,128)S(1)}, u32[]{:S(2)}, u32[]{:S(2)}) collective-permute-start(f32[256,256]{1,0:T(8,128)S(1)} %get-tuple-element.64), channel_id=1, source_target_pairs={{0,32},{32,0},{1,33},{33,1},{2,34},{34,2},{3,35},{35,3},{4,36},{36... | collective-permute-start | bytes 786440 | tf_op jit(solution)/shard_map/ppermute | solution.py:253
  34.6 1.2 %collective-permute-done.2.got_ref = f32[256,256]{1,0:T(8,128)S(1)} collective-permute-done((f32[256,256]{1,0:T(8,128)S(1)}, f32[256,256]{1,0:T(8,128)S(1)}, u32[]{:S(2)}, u32[]{:S(2)}) %collective-permute-start.2) | collective-permute-done | bytes 262176 | tf_op jit(solution)/shard_map/ppermute | solution.py:253
  35.8 0.7 %unswap.1 = (bf16[128,512]{1,0:T(8,128)(2,1)}, bf16[128,512]{1,0:T(8,128)(2,1)}, f32[8,128]{1,0:T(8,128)S(1)}) custom-call(bf16[128,256]{1,0:T(8,128)(2,1)S(1)} %get-tuple-element.59.out_ref, bf16[128,256]{1,0:T(8,128)(2,1)S(1)} %get-tuple-element.63.gx_ref, f32[256,256]{1,0:T(8,128)S(1)} %collective-permute-done.2.got_ref), custom_call_target="tpu_custom_call" | custom-call | tf_op jit(solution)/shard_map/unswap/pallas_call | solution.py:243
  36.5 7.6 %all-to-all-done.1.pieces_ref = f32[32,8,512]{2,1,0:T(8,128)S(1)} async-done(((f32[32,8,512]{2,1,0:T(8,128)}), f32[32,8,512]{2,1,0:T(8,128)S(1)}, u32[]{:S(2)}, u32[]{:S(2)}) %all-to-all-start.1) | async-done | bytes 524320 | tf_op jit(solution)/shard_map/all_to_all | solution.py:280
  44.2 5.4 %collective-permute-start.3 = (f32[4,512]{1,0:T(4,128)S(1)}, f32[4,512]{1,0:T(4,128)S(1)}, u32[]{:S(2)}, u32[]{:S(2)}) collective-permute-start(f32[4,512]{1,0:T(4,128)S(1)} %get-tuple-element.70), channel_id=1, source_target_pairs={{0,32},{32,0},{1,33},{33,1},{2,34},{34,2},{3,35},{35,3},{4,36},{36... | collective-permute-start | bytes 24584 | tf_op jit(solution)/shard_map/ppermute | solution.py:253
  49.6 0.8 %collective-permute-done.3.got_ref = f32[4,512]{1,0:T(4,128)S(1)} collective-permute-done((f32[4,512]{1,0:T(4,128)S(1)}, f32[4,512]{1,0:T(4,128)S(1)}, u32[]{:S(2)}, u32[]{:S(2)}) %collective-permute-start.3) | collective-permute-done | bytes 8224 | tf_op jit(solution)/shard_map/ppermute | solution.py:253
  50.5 0.6 %join.1 = f32[4,2,512]{2,1,0:T(2,128)} custom-call(f32[4,512]{1,0:T(4,128)S(1)} %get-tuple-element.69.keep_ref, f32[4,512]{1,0:T(4,128)S(1)} %collective-permute-done.3.got_ref), custom_call_target="tpu_custom_call" | custom-call | tf_op jit(solution)/shard_map/join/pallas_call | solution.py:243
  (3 shorter events, 0.1 us)
Async XLA Ops:
  0.6 0.9 %copy-start.1 = (bf16[1,128,512]{2,1,0:T(8,128)(2,1)S(1)}, bf16[1,128,512]{2,1,0:T(8,128)(2,1)}, u32[]{:S(2)}) copy-start(bf16[1,128,512]{2,1,0:T(8,128)(2,1)} %param.11) | copy-start | bytes 393220
  0.6 1.0 %copy-start = (bf16[1,128,512]{2,1,0:T(8,128)(2,1)S(1)}, bf16[1,128,512]{2,1,0:T(8,128)(2,1)}, u32[]{:S(2)}) copy-start(bf16[1,128,512]{2,1,0:T(8,128)(2,1)} %param.6) | copy-start | bytes 393220
  0.7 1.0 %copy-start.3 = (f32[512]{0:T(512)S(1)}, f32[512]{0:T(512)}, u32[]{:S(2)}) copy-start(f32[512]{0:T(512)} %param.10) | copy-start | bytes 6148
  0.7 4.4 %copy-start.5 = (bf16[256,2,512]{2,1,0:T(2,128)(2,1)S(1)}, bf16[256,2,512]{2,1,0:T(2,128)(2,1)}, u32[]{:S(2)}) copy-start(bf16[256,2,512]{2,1,0:T(2,128)(2,1)} %param.8) | copy-start | bytes 1572868
  0.7 0.9 %copy-start.2 = (f32[2,512]{1,0:T(2,128)S(1)}, f32[2,512]{1,0:T(2,128)}, u32[]{:S(2)}) copy-start(f32[2,512]{1,0:T(2,128)} %bias_ref.5) | copy-start | bytes 12292
  0.7 0.9 %copy-start.4 = (s32[1,128]{1,0:T(1,128)S(1)}, s32[1,128]{1,0:T(1,128)}, u32[]{:S(2)}) copy-start(s32[1,128]{1,0:T(1,128)} %doc_ref.1) | copy-start | bytes 1540
  1.7 4.5 %collective-permute-start = (f32[264,256]{1,0:T(8,128)S(1)}, f32[264,256]{1,0:T(8,128)S(1)}, u32[]{:S(2)}, u32[]{:S(2)}) collective-permute-start(f32[264,256]{1,0:T(8,128)S(1)} %get-tuple-element.37), channel_id=1, source_target_pairs={{0,32},{32,0},{1,33},{33,1},{2,34},{34,2},{3,35},{35,3},{4,36},{36... | collective-permute-start | bytes 811016 | tf_op jit(solution)/shard_map/ppermute | solution.py:253
  5.0 2.5 %collective-permute-start.1 = (f32[8,128]{1,0:T(8,128)S(1)}, f32[8,128]{1,0:T(8,128)S(1)}, u32[]{:S(2)}, u32[]{:S(2)}) collective-permute-start(f32[8,128]{1,0:T(8,128)S(1)} %head.1.order_ref), channel_id=1, source_target_pairs={{0,4},{4,0},{8,12},{12,8},{16,20},{20,16},{24,28},{28,24},{1,5},{5... | collective-permute-start | bytes 12296 | tf_op jit(solution)/shard_map/ppermute | solution.py:265
  27.2 16.9 %all-to-all-start.1 = ((f32[32,8,512]{2,1,0:T(8,128)}), f32[32,8,512]{2,1,0:T(8,128)S(1)}, u32[]{:S(2)}, u32[]{:S(2)}) async-start(f32[32,8,512]{2,1,0:T(8,128)} %get-tuple-element.67), calls=%async_computation.1 | async-start | bytes 1048576 | tf_op jit(solution)/shard_map/all_to_all | solution.py:280
  32.1 3.7 %collective-permute-start.2 = (f32[256,256]{1,0:T(8,128)S(1)}, f32[256,256]{1,0:T(8,128)S(1)}, u32[]{:S(2)}, u32[]{:S(2)}) collective-permute-start(f32[256,256]{1,0:T(8,128)S(1)} %get-tuple-element.64), channel_id=1, source_target_pairs={{0,32},{32,0},{1,33},{33,1},{2,34},{34,2},{3,35},{35,3},{4,36},{36... | collective-permute-start | bytes 786440 | tf_op jit(solution)/shard_map/ppermute | solution.py:253
  44.2 6.3 %collective-permute-start.3 = (f32[4,512]{1,0:T(4,128)S(1)}, f32[4,512]{1,0:T(4,128)S(1)}, u32[]{:S(2)}, u32[]{:S(2)}) collective-permute-start(f32[4,512]{1,0:T(4,128)S(1)} %get-tuple-element.70), channel_id=1, source_target_pairs={{0,32},{32,0},{1,33},{33,1},{2,34},{34,2},{3,35},{35,3},{4,36},{36... | collective-permute-start | bytes 24584 | tf_op jit(solution)/shard_map/ppermute | solution.py:253

commit v5 on v2

--- a/solution.py
+++ b/solution.py
@@ -261,7 +261,7 @@
     tiles = half // LANES
     summary, *own = call(own_kernel, (own, *gates), [shape((3, tiles, LANES), F32)] + fields, "own_scans")
     summary, *got = call(got_kernel, (got, *gates, summary), [shape((3, 2 * tiles, LANES), F32)] + fields, "got_scans")
-    met = lax.ppermute(order, "z", [(i, i ^ 1) for i in range(n_z)])
+    met = lax.ppermute(order, "x", [(i, i ^ 1) for i in range(n_x)])
     spread = call(spread_kernel, (summary, met), shape((chips, 3, 2 * tiles, LANES), F32), "spread")
     everyone = lax.all_to_all(spread, ("x", "z"), 0, 0)
     out, states, dpre, direct, gw = call(

time: 51.3 us -> 51.3 us (level)
  no operation moved by 1% of the time
where the time goes in v5:
time: 51.3 us; the launch traced here: 51.1 us
  blocking collectives  18.5 us (36%)
  starting transfers between devices  15.9 us (31%)
  waiting for transfers between devices  10.9 us (21%)
  Pallas kernels  4.12 us (8%)
  local copies, waits for them, and re-layouts  0.99 us (2%)
  between operations  0.74 us (1%)
    all_to_all x1, blocking collectives, per_device(): everyone = lax.all_to_all(spread, ('x', 'z'), 0, 0)  18.5 us
    ppermute x3, starting transfers between devices, per_device(): swap = lambda value: lax.ppermute(value, 'core', [(0, 1), (1, 0)])  11.3 us
    all_to_all x1, waiting for transfers between devices, per_device(): pieces = lax.all_to_all(gw, ('x', 'z'), 0, 0)  7.63 us
    all_to_all x1, starting transfers between devices, per_device(): pieces = lax.all_to_all(gw, ('x', 'z'), 0, 0)  4.53 us
    pallas_call x10, Pallas kernels, call(): pl.pallas_call(kernel, out_shape=outs, in_specs=[vmem] * len(operands), s...  4.12 us
    ppermute x3, waiting for transfers between devices, per_device(): swap = lambda value: lax.ppermute(value, 'core', [(0, 1), (1, 0)])  2.52 us
  transfers between devices with their start and end apart: 5, of which 5 were waited for; matrix products, arithmetic and copies ran while one was open for 0% of the time, Pallas kernels for 4%

profile of v5, /device:TPU:1, one launch (start us, length us, event | category | flops | bytes accessed | tf_op | source)
XLA Modules:
  0.0 51.1 jit_solution(13191780848330210474)
XLA Ops:
  0.6 0.0 copy-start.1
  0.6 0.0 copy-start
  0.7 0.0 copy-start.3
  0.7 0.0 copy-start.5
  0.7 0.0 copy-start.2
  0.7 0.0 copy-start.4
  0.7 0.8 %copy-done.1 = bf16[1,128,512]{2,1,0:T(8,128)(2,1)S(1)} copy-done((bf16[1,128,512]{2,1,0:T(8,128)(2,1)S(1)}, bf16[1,128,512]{2,1,0:T(8,128)(2,1)}, u32[]{:S(2)}) %copy-start.1) | copy-done | bytes 131096
  1.5 0.1 copy-done
  1.6 0.0 copy-done.3
  1.6 0.0 copy-done.2
  1.6 0.0 copy-done.4
  1.6 0.1 pack.1
  1.7 3.3 %collective-permute-start = (f32[264,256]{1,0:T(8,128)S(1)}, f32[264,256]{1,0:T(8,128)S(1)}, u32[]{:S(2)}, u32[]{:S(2)}) collective-permute-start(f32[264,256]{1,0:T(8,128)S(1)} %get-tuple-element.37), channel_id=1, source_target_pairs={{0,32},{32,0},{1,33},{33,1},{2,34},{34,2},{3,35},{35,3},{4,36},{36... | collective-permute-start | bytes 811016 | tf_op jit(solution)/shard_map/ppermute | solution.py:252
  5.0 0.0 collective-permute-start.1
  5.0 0.0 copy-done.5
  5.0 0.1 copy.11
  5.1 0.6 %own_scans.1 = (f32[3,2,128]{2,1,0:T(2,128)S(1)}, bf16[128,256]{1,0:T(8,128)(2,1)S(1)}, f32[128,256]{1,0:T(8,128)S(1)}, f32[128,256]{1,0:T(8,128)S(1)}, f32[128,...) custom-call(f32[264,256]{1,0:T(8,128)S(1)} %get-tuple-element.38.pac, ...), custom_call_target="tpu_custom_call" | custom-call | tf_op jit(solution)/shard_map/own_scans/pallas_call | solution.py:242
  5.7 0.5 %collective-permute-done.pack_ref = f32[264,256]{1,0:T(8,128)S(1)} collective-permute-done((f32[264,256]{1,0:T(8,128)S(1)}, f32[264,256]{1,0:T(8,128)S(1)}, u32[]{:S(2)}, u32[]{:S(2)}) %collective-permute-start) | collective-permute-done | bytes 270368 | tf_op jit(solution)/shard_map/ppermute | solution.py:252
  6.2 0.6 %got_scans.1 = (f32[3,4,128]{2,1,0:T(4,128)S(1)}, bf16[128,256]{1,0:T(8,128)(2,1)S(1)}, f32[128,256]{1,0:T(8,128)S(1)}, f32[128,256]{1,0:T(8,128)S(1)}, f32[128,...) custom-call(f32[264,256]{1,0:T(8,128)S(1)} %collective-permute-done., ...), custom_call_target="tpu_custom_call" | custom-call | tf_op jit(solution)/shard_map/got_scans/pallas_call | solution.py:242
  6.8 0.7 %collective-permute-done.1._ = f32[8,128]{1,0:T(8,128)S(1)} collective-permute-done((f32[8,128]{1,0:T(8,128)S(1)}, f32[8,128]{1,0:T(8,128)S(1)}, u32[]{:S(2)}, u32[]{:S(2)}) %collective-permute-start.1) | collective-permute-done | bytes 4128 | tf_op jit(solution)/shard_map/ppermute | solution.py:264
  7.5 18.5 %all_to_all.10.refs_0_ = f32[32,3,4,128]{3,2,1,0:T(4,128)S(1)} all-to-all(f32[32,3,4,128]{3,2,1,0:T(4,128)S(1)} %spread.1), channel_id=1, replica_groups=mesh['x'=4,'core'=2,'z'=8,'mp'=4] {'x','z'}, dimensions={0} | all-to-all | bytes 393216 | tf_op jit(solution)/shard_map/all_to_all | solution.py:266
  26.0 1.2 %finish.1 = (bf16[128,256]{1,0:T(8,128)(2,1)S(1)}, f32[128,256]{1,0:T(8,128)S(1)}, bf16[256,512]{1,0:T(8,128)(2,1)S(1)}, f32[256,256]{1,0:T(8,128)S(1)}, f32[32,8,512]{2,1,0:T(8,128)}) custom-call(f32[32,3,4,128]{3,2,1,0:T(4,128)S(1)} %all_to_all.10.refs_0_, bf16[128,256]{1,0:T(8,128)(2,1)S(1)} %get-tuple-element.41.refs_1_, ...), custom_call_target="tpu_custom_call" | custom-call | tf_op jit(solution)/shard_map/finish/pallas_call | solution.py:242
  27.2 4.5 %all-to-all-start.1 = ((f32[32,8,512]{2,1,0:T(8,128)}), f32[32,8,512]{2,1,0:T(8,128)S(1)}, u32[]{:S(2)}, u32[]{:S(2)}) async-start(f32[32,8,512]{2,1,0:T(8,128)} %get-tuple-element.67), calls=%async_computation.1 | async-start | bytes 1048576 | tf_op jit(solution)/shard_map/all_to_all | solution.py:279
  31.8 0.3 grad_inputs.1
  32.1 2.6 %collective-permute-start.2 = (f32[256,256]{1,0:T(8,128)S(1)}, f32[256,256]{1,0:T(8,128)S(1)}, u32[]{:S(2)}, u32[]{:S(2)}) collective-permute-start(f32[256,256]{1,0:T(8,128)S(1)} %get-tuple-element.64), channel_id=1, source_target_pairs={{0,32},{32,0},{1,33},{33,1},{2,34},{34,2},{3,35},{35,3},{4,36},{36... | collective-permute-start | bytes 786440 | tf_op jit(solution)/shard_map/ppermute | solution.py:252
  34.6 1.2 %collective-permute-done.2.got_ref = f32[256,256]{1,0:T(8,128)S(1)} collective-permute-done((f32[256,256]{1,0:T(8,128)S(1)}, f32[256,256]{1,0:T(8,128)S(1)}, u32[]{:S(2)}, u32[]{:S(2)}) %collective-permute-start.2) | collective-permute-done | bytes 262176 | tf_op jit(solution)/shard_map/ppermute | solution.py:252
  35.8 0.7 %unswap.1 = (bf16[128,512]{1,0:T(8,128)(2,1)}, bf16[128,512]{1,0:T(8,128)(2,1)}, f32[8,128]{1,0:T(8,128)S(1)}) custom-call(bf16[128,256]{1,0:T(8,128)(2,1)S(1)} %get-tuple-element.59.out_ref, bf16[128,256]{1,0:T(8,128)(2,1)S(1)} %get-tuple-element.63.gx_ref, f32[256,256]{1,0:T(8,128)S(1)} %collective-permute-done.2.got_ref), custom_call_target="tpu_custom_call" | custom-call | tf_op jit(solution)/shard_map/unswap/pallas_call | solution.py:242
  36.5 7.6 %all-to-all-done.1.pieces_ref = f32[32,8,512]{2,1,0:T(8,128)S(1)} async-done(((f32[32,8,512]{2,1,0:T(8,128)}), f32[32,8,512]{2,1,0:T(8,128)S(1)}, u32[]{:S(2)}, u32[]{:S(2)}) %all-to-all-start.1) | async-done | bytes 524320 | tf_op jit(solution)/shard_map/all_to_all | solution.py:279
  44.2 5.4 %collective-permute-start.3 = (f32[4,512]{1,0:T(4,128)S(1)}, f32[4,512]{1,0:T(4,128)S(1)}, u32[]{:S(2)}, u32[]{:S(2)}) collective-permute-start(f32[4,512]{1,0:T(4,128)S(1)} %get-tuple-element.70), channel_id=1, source_target_pairs={{0,32},{32,0},{1,33},{33,1},{2,34},{34,2},{3,35},{35,3},{4,36},{36... | collective-permute-start | bytes 24584 | tf_op jit(solution)/shard_map/ppermute | solution.py:252
  49.6 0.8 %collective-permute-done.3.got_ref = f32[4,512]{1,0:T(4,128)S(1)} collective-permute-done((f32[4,512]{1,0:T(4,128)S(1)}, f32[4,512]{1,0:T(4,128)S(1)}, u32[]{:S(2)}, u32[]{:S(2)}) %collective-permute-start.3) | collective-permute-done | bytes 8224 | tf_op jit(solution)/shard_map/ppermute | solution.py:252
  50.5 0.6 %join.1 = f32[4,2,512]{2,1,0:T(2,128)} custom-call(f32[4,512]{1,0:T(4,128)S(1)} %get-tuple-element.69.keep_ref, f32[4,512]{1,0:T(4,128)S(1)} %collective-permute-done.3.got_ref), custom_call_target="tpu_custom_call" | custom-call | tf_op jit(solution)/shard_map/join/pallas_call | solution.py:242
  (3 shorter events, 0.1 us)
Async XLA Ops:
  0.6 0.9 %copy-start.1 = (bf16[1,128,512]{2,1,0:T(8,128)(2,1)S(1)}, bf16[1,128,512]{2,1,0:T(8,128)(2,1)}, u32[]{:S(2)}) copy-start(bf16[1,128,512]{2,1,0:T(8,128)(2,1)} %param.11) | copy-start | bytes 393220
  0.6 1.0 %copy-start = (bf16[1,128,512]{2,1,0:T(8,128)(2,1)S(1)}, bf16[1,128,512]{2,1,0:T(8,128)(2,1)}, u32[]{:S(2)}) copy-start(bf16[1,128,512]{2,1,0:T(8,128)(2,1)} %param.6) | copy-start | bytes 393220
  0.7 1.0 %copy-start.3 = (f32[512]{0:T(512)S(1)}, f32[512]{0:T(512)}, u32[]{:S(2)}) copy-start(f32[512]{0:T(512)} %param.10) | copy-start | bytes 6148
  0.7 4.4 %copy-start.5 = (bf16[256,2,512]{2,1,0:T(2,128)(2,1)S(1)}, bf16[256,2,512]{2,1,0:T(2,128)(2,1)}, u32[]{:S(2)}) copy-start(bf16[256,2,512]{2,1,0:T(2,128)(2,1)} %param.8) | copy-start | bytes 1572868
  0.7 0.9 %copy-start.2 = (f32[2,512]{1,0:T(2,128)S(1)}, f32[2,512]{1,0:T(2,128)}, u32[]{:S(2)}) copy-start(f32[2,512]{1,0:T(2,128)} %bias_ref.5) | copy-start | bytes 12292
  0.7 0.9 %copy-start.4 = (s32[1,128]{1,0:T(1,128)S(1)}, s32[1,128]{1,0:T(1,128)}, u32[]{:S(2)}) copy-start(s32[1,128]{1,0:T(1,128)} %doc_ref.1) | copy-start | bytes 1540
  1.7 4.5 %collective-permute-start = (f32[264,256]{1,0:T(8,128)S(1)}, f32[264,256]{1,0:T(8,128)S(1)}, u32[]{:S(2)}, u32[]{:S(2)}) collective-permute-start(f32[264,256]{1,0:T(8,128)S(1)} %get-tuple-element.37), channel_id=1, source_target_pairs={{0,32},{32,0},{1,33},{33,1},{2,34},{34,2},{3,35},{35,3},{4,36},{36... | collective-permute-start | bytes 811016 | tf_op jit(solution)/shard_map/ppermute | solution.py:252
  5.0 2.5 %collective-permute-start.1 = (f32[8,128]{1,0:T(8,128)S(1)}, f32[8,128]{1,0:T(8,128)S(1)}, u32[]{:S(2)}, u32[]{:S(2)}) collective-permute-start(f32[8,128]{1,0:T(8,128)S(1)} %head.1.order_ref), channel_id=1, source_target_pairs={{0,64},{64,0},{128,192},{192,128},{1,65},{65,1},{129,193},{193,129... | collective-permute-start | bytes 12296 | tf_op jit(solution)/shard_map/ppermute | solution.py:264
  27.2 16.9 %all-to-all-start.1 = ((f32[32,8,512]{2,1,0:T(8,128)}), f32[32,8,512]{2,1,0:T(8,128)S(1)}, u32[]{:S(2)}, u32[]{:S(2)}) async-start(f32[32,8,512]{2,1,0:T(8,128)} %get-tuple-element.67), calls=%async_computation.1 | async-start | bytes 1048576 | tf_op jit(solution)/shard_map/all_to_all | solution.py:279
  32.1 3.7 %collective-permute-start.2 = (f32[256,256]{1,0:T(8,128)S(1)}, f32[256,256]{1,0:T(8,128)S(1)}, u32[]{:S(2)}, u32[]{:S(2)}) collective-permute-start(f32[256,256]{1,0:T(8,128)S(1)} %get-tuple-element.64), channel_id=1, source_target_pairs={{0,32},{32,0},{1,33},{33,1},{2,34},{34,2},{3,35},{35,3},{4,36},{36... | collective-permute-start | bytes 786440 | tf_op jit(solution)/shard_map/ppermute | solution.py:252
  44.2 6.3 %collective-permute-start.3 = (f32[4,512]{1,0:T(4,128)S(1)}, f32[4,512]{1,0:T(4,128)S(1)}, u32[]{:S(2)}, u32[]{:S(2)}) collective-permute-start(f32[4,512]{1,0:T(4,128)S(1)} %get-tuple-element.70), channel_id=1, source_target_pairs={{0,32},{32,0},{1,33},{33,1},{2,34},{34,2},{3,35},{35,3},{4,36},{36... | collective-permute-start | bytes 24584 | tf_op jit(solution)/shard_map/ppermute | solution.py:252
